TPU v7x, 128 devices: a whole 4x4x4 slice. The times are simulated.
128 devices in a mesh: space: 32 (over y, z, core), scene: 4 (over x).
Axes of the slice: x: 4, y: 4, z: 4, core: 2. Of those that a mesh axis runs over, the one named last changes fastest.
Arguments:
- feats: bfloat16 [1024, 512, 128], P(('scene', 'space')), parts along dimension 0, may hold values from -6 to 6
- mask: int32 [1024, 512], P(('scene', 'space')), parts along dimension 0, may hold values from 0 to 1, as said below
- neighbours: int32 [1024, 8], P(('scene', 'space')), parts along dimension 0, may hold values from -1 to 255, as said below
- weight_one: bfloat16 [27, 128, 128], replicated, may hold values from -0.109375 to 0.109375
- weight_two: bfloat16 [27, 128, 128], replicated, may hold values from -0.109375 to 0.109375
- cotangent: bfloat16 [1024, 512, 128], P(('scene', 'space')), parts along dimension 0, may hold values from -12 to 12
Outputs:
- output: bfloat16 [1024, 512, 128], P(('scene', 'space')), parts along dimension 0
- grad_input: bfloat16 [1024, 512, 128], P(('scene', 'space')), parts along dimension 0
- grad_w1: float32 [108, 128, 128], P('scene'), parts along dimension 0
- grad_w2: float32 [108, 128, 128], P('scene'), parts along dimension 0
There are 4 independent parts, one for each index of `scene`. A program takes and returns all parts, laid end to end along the dimension named above; an argument that names none is the same for every part. Nothing has to cross between parts.
Inputs may be any that keep to these rules, and one draw needn't show every extreme that they name: `mask`: 1 where the voxel is occupied, else 0; an empty brick (see neighbours) is 0 throughout. `neighbours`: A brick number or -1. Brick g is held by index g // 8 of space, and the entries of brick g name only bricks held by that index or by the index one lower or one higher. If brick g names brick h in a direction, h names g in the opposite one (entry 7 - j for entry j). Empty bricks have only -1 entries and are named by no entry. Brick 256 - 1 is named in every draw.
All inputs are finite; a program needn't handle non-finite values.
Results may differ from a plain program's by a relative error of at most 0.02.
Values may be sent and summed in bfloat16 or wider, within the bound.
A program may use at most 192 MiB of HBM per device.

v0:
```python
import math

import jax
import jax.numpy as jnp
from jax import lax
from jax.sharding import PartitionSpec as P

EDGE = 8
TILE = 1
WIDE = 8


DIRECTIONS = ((-1, -1), (-1, 0), (-1, 1), (0, -1), (0, 1), (1, -1), (1, 0), (1, 1))


def padded_2(cells, sides, width):
    for axis, dim in sides:
        count = lax.axis_size(axis)
        ends = count - 1
        head = lax.slice_in_dim(cells, 0, width, axis=dim)
        tail = lax.slice_in_dim(cells, cells.shape[dim] - width, cells.shape[dim], axis=dim)
        cells = jnp.concatenate(
            [
                lax.ppermute(tail, axis, [(i, (i + 1) % count) for i in range(ends)]),
                cells,
                lax.ppermute(head, axis, [((i + 1) % count, i) for i in range(ends)]),
            ],
            axis=dim,
        )
    return cells


def rim_slices(step_value, length):
    if step_value < 0:
        return (slice(length - 1, length), slice(0, 1))
    if step_value > 0:
        return (slice(0, 1), slice(length + 1, length + 2))
    return (slice(0, length), slice(1, length + 1))


def assemble(cube_view, sources, source_index):
    length = cube_view.shape[1]
    padded = jnp.pad(cube_view, ((0, 0), (1, 1), (1, 1), (1, 1), (0, 0)))
    for column, (step_x, step_y) in enumerate(DIRECTIONS):
        source_x, target_x = rim_slices(step_x, length)
        source_y, target_y = rim_slices(step_y, length)
        rim_cells = sources[:, source_x, source_y]
        fetched = jnp.take(rim_cells, source_index[:, column], axis=0)
        padded = padded.at[:, target_x, target_y, 1 : length + 1].set(fetched)
    return padded


def window_stack(padded, shift_x, flipped):
    length = padded.shape[1] - 2
    channels = padded.shape[-1]
    pieces = []
    for shift_y in range(3):
        for shift_z in range(3):
            if flipped:
                corner_x, corner_y, corner_z = (2 - shift_x, 2 - shift_y, 2 - shift_z)
            else:
                corner_x, corner_y, corner_z = (shift_x, shift_y, shift_z)
            cells = padded[
                :,
                corner_x : corner_x + length,
                corner_y : corner_y + length,
                corner_z : corner_z + length,
            ]
            pieces.append(cells.reshape(-1, channels))
    return jnp.concatenate(pieces, axis=1)


def convolve(padded, weight, flipped):
    channels = padded.shape[-1]
    summed = None
    for shift_x in range(3):
        stacked = window_stack(padded, shift_x, flipped)
        weight_block = weight[9 * shift_x : 9 * shift_x + 9]
        if flipped:
            weight_block = jnp.swapaxes(weight_block, 1, 2)
        partial_sum = jnp.dot(
            stacked,
            weight_block.reshape(9 * channels, channels),
            preferred_element_type=jnp.float32,
        )
        summed = partial_sum if summed is None else summed + partial_sum
    return summed


def weight_grad(padded, grads):
    channels = padded.shape[-1]
    blocks = []
    for shift_x in range(3):
        stacked = window_stack(padded, shift_x, False)
        product = lax.dot_general(
            stacked, grads, (((0,), (0,)), ((), ())), preferred_element_type=jnp.float32
        )
        blocks.append(product.reshape(9, channels, channels))
    return jnp.concatenate(blocks, axis=0)


def silu_slope(values):
    sigmoid_value = jax.nn.sigmoid(values)
    return sigmoid_value * (1.0 + values * (1.0 - sigmoid_value))


def body(feats, mask, neighbours, weight_one, weight_two, cotangent):
    bricks, voxels, channels = feats.shape
    my_index = lax.axis_index("space")
    first_brick = (my_index * TILE - 1) * WIDE
    source_index = jnp.where(neighbours >= 0, neighbours - first_brick, (TILE + 2) * WIDE)
    occupied = mask.reshape(-1, 1).astype(jnp.float32)
    blank_brick = jnp.zeros((1, EDGE, EDGE, EDGE, channels), jnp.bfloat16)

    def join_sources(cube_view, left_side, right_side):
        sources = jnp.concatenate([left_side, cube_view, right_side, blank_brick], axis=0)
        return assemble(cube_view, sources, source_index)

    def extend_bricks(flat_field, received):
        cube_view = flat_field.reshape(bricks, EDGE, EDGE, EDGE, channels)
        left_side = received[0].reshape(WIDE, EDGE, EDGE, EDGE, channels)
        right_side = received[TILE + 1].reshape(WIDE, EDGE, EDGE, EDGE, channels)
        return join_sources(cube_view, left_side, right_side)

    def as_tiles(flat_field):
        return flat_field.reshape(TILE, WIDE, voxels, channels)

    inputs = feats * mask[:, :, None].astype(jnp.bfloat16)
    padded_in = extend_bricks(inputs, padded_2(as_tiles(inputs), (("space", 0),), 1))
    first_pre = convolve(padded_in, weight_one, False)
    hidden = (
        (occupied * jax.nn.silu(first_pre)).astype(jnp.bfloat16).reshape(bricks, voxels, channels)
    )
    padded_hidden = extend_bricks(hidden, padded_2(as_tiles(hidden), (("space", 0),), 1))
    second_pre = convolve(padded_hidden, weight_two, False)
    output = (occupied * jax.nn.silu(second_pre)).astype(jnp.bfloat16)
    grad_second = (
        cotangent.reshape(-1, channels).astype(jnp.float32) * occupied * silu_slope(second_pre)
    ).astype(jnp.bfloat16)
    grad_second_view = grad_second.reshape(bricks, voxels, channels)
    padded_second = extend_bricks(
        grad_second_view, padded_2(as_tiles(grad_second_view), (("space", 0),), 1)
    )
    back_second = convolve(padded_second, weight_two, True)
    grad_first = (occupied * silu_slope(first_pre) * back_second).astype(jnp.bfloat16)
    grad_scale = 1.0 / math.sqrt(voxels * bricks)
    grad_w2 = weight_grad(padded_hidden, grad_second) * grad_scale
    grad_w2 = lax.psum(grad_w2.astype(jnp.bfloat16), "space").astype(jnp.float32)
    grad_first_view = grad_first.reshape(bricks, voxels, channels)
    padded_first = extend_bricks(
        grad_first_view, padded_2(as_tiles(grad_first_view), (("space", 0),), 1)
    )
    grad_input = (occupied * convolve(padded_first, weight_one, True)).astype(jnp.bfloat16)
    grad_w1 = weight_grad(padded_in, grad_first) * grad_scale
    grad_w1 = lax.psum(grad_w1.astype(jnp.bfloat16), "space").astype(jnp.float32)
    return (
        output.reshape(bricks, voxels, channels),
        grad_input.reshape(bricks, voxels, channels),
        grad_w1,
        grad_w2,
    )


def solution(mesh):
    in_specs = (
        P(("scene", "space"), None, None),
        P(("scene", "space"), None),
        P(("scene", "space"), None),
        P(),
        P(),
        P(("scene", "space"), None, None),
    )
    out_specs = (
        P(("scene", "space"), None, None),
        P(("scene", "space"), None, None),
        P("scene", None, None),
        P("scene", None, None),
    )
    return jax.shard_map(body, mesh=mesh, in_specs=in_specs, out_specs=out_specs, check_vma=False)
```

profile of v0, /device:TPU:1, one launch (start us, length us, event | category | flops | bytes accessed | tf_op | source)
XLA Modules:
  0.0 491.1 jit_solution(3346100153531538435)
XLA Ops:
  10.5 4.9 %collective-permute-start = (bf16[1,8,512,128]{3,2,1,0:T(8,128)(2,1)}, bf16[1,8,512,128]{3,2,1,0:T(8,128)(2,1)}, u32[]{:S(2)}, u32[]{:S(2)}) collective-permute-start(bf16[1,8,512,128]{3,2,1,0:T(8,128)(2,1)} %fusion.94), channel_id=1, source_target_pairs={{0,4},{4,8},{8,12},{12,16},{16,20},{20,24},{24,28},{28,32},{32,36}... | collective-permute-start | bytes 3145736 | tf_op jit(solution)/shard_map/ppermute | solution.py:24
  58.4 8.1 %fusion.46 = (bf16[8,8,8,8,128]{4,3,2,1,0:T(8,128)(2,1)}, bf16[8,8,8,8,128]{4,3,2,1,0:T(8,128)(2,1)}, bf16[8,8,8,8,128]{4,3,2,1,0:T(8,128)(2,1)}, bf16[8,8,8,8,1...) fusion(bf16[8,10,10,10,128]{4,3,2,1,0:T(8,128)(2,1)S(1)} %scatt, ...), kind=kLoop, calls=%fused_computation.310 | loop fusion | bytes 39845888 | tf_op jit(solution)/shard_map/slice | solution.py:63
  84.0 2.6 fusion.48
  86.6 2.6 convolution_add_fusion.7
  92.1 4.7 multiply_convert_fusion.1
  96.8 3.4 collective-permute-start.2
  108.1 4.2 collective-permute-done.2
  112.3 4.4 collective-permute-done.3
  153.0 8.1 %fusion.44 = (bf16[8,8,8,8,128]{4,3,2,1,0:T(8,128)(2,1)}, bf16[8,8,8,8,128]{4,3,2,1,0:T(8,128)(2,1)}, bf16[8,8,8,8,128]{4,3,2,1,0:T(8,128)(2,1)}, bf16[8,8,8,8,1...) fusion(bf16[8,10,10,10,128]{4,3,2,1,0:T(8,128)(2,1)S(1)} %scatt, ...), kind=kLoop, calls=%fused_computation.308 | loop fusion | bytes 39845888 | tf_op jit(solution)/shard_map/slice | solution.py:63
  178.1 2.7 fusion.49
  180.9 2.7 convolution_add_fusion.5
  183.7 5.0 %fusion.5 = (bf16[4096,128]{1,0:T(8,128)(2,1)S(1)}, bf16[4096,128]{1,0:T(8,128)(2,1)}) fusion(bf16[8,512,128]{2,1,0:T(8,128)(2,1)S(1)} %copy-done.106, f32[4096]{0:T(1024)S(1)} %bitcast.596, f32[4096,128]{1,0:T(8,128)S(1)} %convolution_add_fusion.5, bf16[4096,1152]{1,0:T(8,128)(2,1)S(1)} %bitcast.604, bf16[1152,128]{1,0:T(8,128)(2,1)S(1)} %bitcast.594), kind=kOutput, calls=%fused_computation.50 | convolution fusion | flops 1215823872 | bytes 14991360 | tf_op jit(solution)/shard_map/dot_general | solution.py:81
  188.6 2.7 fusion.57
  195.7 2.7 fusion.56
  199.2 2.7 fusion.55
  204.9 4.7 collective-permute-done.5
  244.4 7.9 %fusion.42 = (bf16[8,8,8,8,128]{4,3,2,1,0:T(8,128)(2,1)}, bf16[8,8,8,8,128]{4,3,2,1,0:T(8,128)(2,1)}, bf16[8,8,8,8,128]{4,3,2,1,0:T(8,128)(2,1)}, bf16[8,8,8,8,1...) fusion(bf16[8,10,10,10,128]{4,3,2,1,0:T(8,128)(2,1)S(1)} %scatt, ...), kind=kLoop, calls=%fused_computation.306 | loop fusion | bytes 39845888 | tf_op jit(solution)/shard_map/slice | solution.py:63
  265.3 2.6 fusion.50
  268.0 2.9 convolution_add_fusion.3
  270.9 8.5 %fusion.2 = bf16[4096,128]{1,0:T(8,128)(2,1)} fusion(f32[4096,128]{1,0:T(8,128)S(1)} %convolution_add_fusion.3, bf16[4096,1152]{1,0:T(8,128)(2,1)} %copy-done.95, bf16[1152,128]{1,0:T(8,128)(2,1)S(1)} %bitcast.592, f32[4096,128]{1,0:T(8,128)S(1)} %copy-done.107, f32[4096]{0:T(1024)S(1)} %bitcast.597), kind=kOutput, calls=%fused_computation.42 | convolution fusion | flops 1213726720 | bytes 14991360 | tf_op jit(solution)/shard_map/dot_general | solution.py:81
  279.5 4.0 fusion.54
  283.5 4.0 fusion.53
  289.6 3.8 collective-permute-start.7
  293.5 3.9 fusion.52
  303.2 107.1 %all-reduce.7.cloned.1.call-done = (bf16[27,128,128]{2,1,0:T(8,128)(2,1)}, bf16[27,128,128]{2,1,0:T(8,128)(2,1)}) async-done(((bf16[27,128,128]{2,1,0:T(8,128)(2,1)}, bf16[27,128,128]{2,1,0:T(8,128)(2,1)}), (bf16[27,128,128]{2,1,0:T(8,128)(2,1)}, bf16[27,128,128]{2,1,0:T(8,128)(2,1)})) %all-reduce.7.cloned.1.call-update) | async-done | bytes 1769488 | tf_op jit(solution)/shard_map/psum | solution.py:155
  410.3 2.6 convert_element_type.64
  412.9 2.6 convert_element_type.66
  451.9 8.1 %fusion.40 = (bf16[8,8,8,8,128]{4,3,2,1,0:T(8,128)(2,1)}, bf16[8,8,8,8,128]{4,3,2,1,0:T(8,128)(2,1)}, bf16[8,8,8,8,128]{4,3,2,1,0:T(8,128)(2,1)}, bf16[8,8,8,8,1...) fusion(bf16[8,10,10,10,128]{4,3,2,1,0:T(8,128)(2,1)S(1)} %scatt, ...), kind=kLoop, calls=%fused_computation.304 | loop fusion | bytes 39845888 | tf_op jit(solution)/shard_map/slice | solution.py:63
  459.9 3.3 fusion.41
  474.8 2.6 fusion.51
  477.4 2.9 convolution_add_fusion.1
  480.3 3.7 fusion.3
  (523 shorter events, 237.5 us)
Async XLA Ops:
  7.2 403.2 %all-reduce.7.cloned.1.call-start = ((), (), s32[]{:S(2)}) async-start(), calls=%async_computation | async-start | bytes 3538944 | tf_op jit(solution)/shard_map/psum | solution.py:155
  10.5 21.0 %collective-permute-start = (bf16[1,8,512,128]{3,2,1,0:T(8,128)(2,1)}, bf16[1,8,512,128]{3,2,1,0:T(8,128)(2,1)}, u32[]{:S(2)}, u32[]{:S(2)}) collective-permute-start(bf16[1,8,512,128]{3,2,1,0:T(8,128)(2,1)} %fusion.94), channel_id=1, source_target_pairs={{0,4},{4,8},{8,12},{12,16},{16,20},{20,24},{24,28},{28,32},{32,36}... | collective-permute-start | bytes 3145736 | tf_op jit(solution)/shard_map/ppermute | solution.py:24
  15.5 16.4 %collective-permute-start.1 = (bf16[1,8,512,128]{3,2,1,0:T(8,128)(2,1)}, bf16[1,8,512,128]{3,2,1,0:T(8,128)(2,1)}, u32[]{:S(2)}, u32[]{:S(2)}) collective-permute-start(bf16[1,8,512,128]{3,2,1,0:T(8,128)(2,1)} %fusion.94), channel_id=1, source_target_pairs={{4,0},{8,4},{12,8},{16,12},{20,16},{24,20},{28,24},{32,28},{36,32}... | collective-permute-start | bytes 3145736 | tf_op jit(solution)/shard_map/ppermute | solution.py:26
  21.5 18.0 %copy-start.96 = (pred[8]{0:T(512)(128)(4,1)}, pred[8]{0:T(512)(128)(4,1)S(1)}, u32[]{:S(2)}) copy-start(pred[8]{0:T(512)(128)(4,1)S(1)} %get-tuple-element.574) | copy-start | bytes 28
  21.5 18.0 %copy-start.101 = (s32[1024]{0:T(1024)}, s32[1024]{0:T(1024)S(1)}, u32[]{:S(2)}) copy-start(s32[1024]{0:T(1024)S(1)} %pad_clamp_fusion.7) | copy-start | bytes 12292
  21.6 18.0 %copy-start.100 = (s32[1024]{0:T(1024)}, s32[1024]{0:T(1024)S(1)}, u32[]{:S(2)}) copy-start(s32[1024]{0:T(1024)S(1)} %pad_clamp_fusion.6) | copy-start | bytes 12292
  70.4 9.3 %copy-start.37 = (bf16[8,8,8,8,128]{4,3,2,1,0:T(8,128)(2,1)S(1)}, bf16[8,8,8,8,128]{4,3,2,1,0:T(8,128)(2,1)}, u32[]{:S(2)}) copy-start(bf16[8,8,8,8,128]{4,3,2,1,0:T(8,128)(2,1)} %get-tuple-element.522) | copy-start | bytes 3145732
  70.6 9.3 %copy-start.33 = (bf16[8,8,8,8,128]{4,3,2,1,0:T(8,128)(2,1)S(1)}, bf16[8,8,8,8,128]{4,3,2,1,0:T(8,128)(2,1)}, u32[]{:S(2)}) copy-start(bf16[8,8,8,8,128]{4,3,2,1,0:T(8,128)(2,1)} %get-tuple-element.521) | copy-start | bytes 3145732
  92.1 10.2 %copy-start.91 = (bf16[27,128,128]{2,1,0:T(8,128)(2,1)S(1)}, bf16[27,128,128]{2,1,0:T(8,128)(2,1)}, u32[]{:S(2)}) copy-start(bf16[27,128,128]{2,1,0:T(8,128)(2,1)} %param.80) | copy-start | bytes 2654212
  92.1 24.6 %copy-start.103 = (bf16[25]{0:T(256)(128)(2,1)S(1)}, bf16[25]{0:T(256)(128)(2,1)}, u32[]{:S(2)}) copy-start(bf16[25]{0:T(256)(128)(2,1)} %copy-done.102) | copy-start | bytes 154
  96.8 25.4 %copy-start.97 = (pred[8]{0:T(512)(128)(4,1)S(1)}, pred[8]{0:T(512)(128)(4,1)}, u32[]{:S(2)}) copy-start(pred[8]{0:T(512)(128)(4,1)} %copy-done.96) | copy-start | bytes 28
  96.8 15.5 %collective-permute-start.2 = (bf16[1,8,512,128]{3,2,1,0:T(8,128)(2,1)}, bf16[1,8,512,128]{3,2,1,0:T(8,128)(2,1)}, u32[]{:S(2)}, u32[]{:S(2)}) collective-permute-start(bf16[1,8,512,128]{3,2,1,0:T(8,128)(2,1)} %bitcast.59), channel_id=1, source_target_pairs={{0,4},{4,8},{8,12},{12,16},{16,20},{20,24},{24,28},{28,32},{32,36}... | collective-permute-start | bytes 3145736 | tf_op jit(solution)/shard_map/ppermute | solution.py:24
  100.2 16.4 %collective-permute-start.3 = (bf16[1,8,512,128]{3,2,1,0:T(8,128)(2,1)}, bf16[1,8,512,128]{3,2,1,0:T(8,128)(2,1)}, u32[]{:S(2)}, u32[]{:S(2)}) collective-permute-start(bf16[1,8,512,128]{3,2,1,0:T(8,128)(2,1)} %bitcast.59), channel_id=1, source_target_pairs={{4,0},{8,4},{12,8},{16,12},{20,16},{24,20},{28,24},{32,28},{36,32}... | collective-permute-start | bytes 3145736 | tf_op jit(solution)/shard_map/ppermute | solution.py:26
  191.3 13.7 %collective-permute-start.4 = (bf16[1,8,512,128]{3,2,1,0:T(8,128)(2,1)S(1)}, bf16[1,8,512,128]{3,2,1,0:T(8,128)(2,1)S(1)}, u32[]{:S(2)}, u32[]{:S(2)}) collective-permute-start(bf16[1,8,512,128]{3,2,1,0:T(8,128)(2,1)S(1)} %bitcast.462), channel_id=1, source_target_pairs={{0,4},{4,8},{8,12},{12,16},{16,20},{20,24},{24,28},{28,32},{32,36}... | collective-permute-start | bytes 3145736 | tf_op jit(solution)/shard_map/ppermute | solution.py:24
  193.2 16.4 %collective-permute-start.5 = (bf16[1,8,512,128]{3,2,1,0:T(8,128)(2,1)S(1)}, bf16[1,8,512,128]{3,2,1,0:T(8,128)(2,1)S(1)}, u32[]{:S(2)}, u32[]{:S(2)}) collective-permute-start(bf16[1,8,512,128]{3,2,1,0:T(8,128)(2,1)S(1)} %bitcast.463), channel_id=1, source_target_pairs={{4,0},{8,4},{12,8},{16,12},{20,16},{24,20},{28,24},{32,28},{36,32}... | collective-permute-start | bytes 3145736 | tf_op jit(solution)/shard_map/ppermute | solution.py:26
  198.4 11.3 %copy-start.104 = (bf16[25]{0:T(256)(128)(2,1)S(1)}, bf16[25]{0:T(256)(128)(2,1)}, u32[]{:S(2)}) copy-start(bf16[25]{0:T(256)(128)(2,1)} %copy-done.102) | copy-start | bytes 154
  199.2 14.4 %copy-start.98 = (pred[8]{0:T(512)(128)(4,1)S(1)}, pred[8]{0:T(512)(128)(4,1)}, u32[]{:S(2)}) copy-start(pred[8]{0:T(512)(128)(4,1)} %copy-done.96) | copy-start | bytes 28
  268.0 11.4 %slice-start.9 = ((s8[9437184]{0:T(1024)(128)(4,1)}), s8[4194304]{0:T(1024)(128)(4,1)S(1)}, s32[]{:S(2)}) async-start(s8[9437184]{0:T(1024)(128)(4,1)} %bitcast.601), calls=%async_computation.10 | async-start | bytes 8388608
  268.0 11.4 %slice-start.10 = ((s8[9437184]{0:T(1024)(128)(4,1)}), s8[4194304]{0:T(1024)(128)(4,1)S(1)}, s32[]{:S(2)}) async-start(s8[9437184]{0:T(1024)(128)(4,1)} %bitcast.601), calls=%async_computation.11 | async-start | bytes 8388608
  268.0 15.5 %slice-start = ((s8[9437184]{0:T(1024)(128)(4,1)}), s8[4194304]{0:T(1024)(128)(4,1)S(1)}, s32[]{:S(2)}) async-start(s8[9437184]{0:T(1024)(128)(4,1)} %bitcast.456), calls=%async_computation.1 | async-start | bytes 8388608
  268.0 15.5 %slice-start.1 = ((s8[9437184]{0:T(1024)(128)(4,1)}), s8[4194304]{0:T(1024)(128)(4,1)S(1)}, s32[]{:S(2)}) async-start(s8[9437184]{0:T(1024)(128)(4,1)} %bitcast.456), calls=%async_computation.2 | async-start | bytes 8388608
  270.9 12.6 %slice-start.2 = ((s8[9437184]{0:T(1024)(128)(4,1)}), s8[1048576]{0:T(1024)(128)(4,1)S(1)}, s32[]{:S(2)}) async-start(s8[9437184]{0:T(1024)(128)(4,1)} %bitcast.456), calls=%async_computation.3 | async-start | bytes 2097152
  279.4 14.0 %slice-start.3 = ((s8[9437184]{0:T(1024)(128)(4,1)}), s8[4194304]{0:T(1024)(128)(4,1)S(1)}, s32[]{:S(2)}) async-start(s8[9437184]{0:T(1024)(128)(4,1)} %bitcast.458), calls=%async_computation.4 | async-start | bytes 8388608
  279.5 14.0 %slice-start.4 = ((s8[9437184]{0:T(1024)(128)(4,1)}), s8[4194304]{0:T(1024)(128)(4,1)S(1)}, s32[]{:S(2)}) async-start(s8[9437184]{0:T(1024)(128)(4,1)} %bitcast.458), calls=%async_computation.5 | async-start | bytes 8388608
  283.5 9.9 %slice-start.5 = ((s8[9437184]{0:T(1024)(128)(4,1)}), s8[1048576]{0:T(1024)(128)(4,1)S(1)}, s32[]{:S(2)}) async-start(s8[9437184]{0:T(1024)(128)(4,1)} %bitcast.458), calls=%async_computation.6 | async-start | bytes 2097152
  287.5 11.0 %copy-start.85 = (bf16[9,128,128]{1,2,0:T(8,128)(2,1)S(1)}, bf16[9,128,128]{1,2,0:T(8,128)(2,1)}, u32[]{:S(2)}) copy-start(bf16[9,128,128]{1,2,0:T(8,128)(2,1)} %get-tuple-element.544) | copy-start | bytes 884740
  287.5 11.9 %copy-start.84 = (bf16[9,128,128]{1,2,0:T(8,128)(2,1)S(1)}, bf16[9,128,128]{1,2,0:T(8,128)(2,1)}, u32[]{:S(2)}) copy-start(bf16[9,128,128]{1,2,0:T(8,128)(2,1)} %get-tuple-element.545) | copy-start | bytes 884740
  287.5 12.8 %copy-start.83 = (bf16[9,128,128]{1,2,0:T(8,128)(2,1)S(1)}, bf16[9,128,128]{1,2,0:T(8,128)(2,1)}, u32[]{:S(2)}) copy-start(bf16[9,128,128]{1,2,0:T(8,128)(2,1)} %get-tuple-element.543) | copy-start | bytes 884740
  287.5 127.9 %collective-permute-start.6 = (bf16[1,8,512,128]{3,2,1,0:T(8,128)(2,1)}, bf16[1,8,512,128]{3,2,1,0:T(8,128)(2,1)}, u32[]{:S(2)}, u32[]{:S(2)}) collective-permute-start(bf16[1,8,512,128]{3,2,1,0:T(8,128)(2,1)} %bitcast.180), channel_id=1, source_target_pairs={{0,4},{4,8},{8,12},{12,16},{16,20},{20,24},{24,28},{28,32},{32,36}... | collective-permute-start | bytes 3145736 | tf_op jit(solution)/shard_map/ppermute | solution.py:24
  289.6 125.9 %collective-permute-start.7 = (bf16[1,8,512,128]{3,2,1,0:T(8,128)(2,1)}, bf16[1,8,512,128]{3,2,1,0:T(8,128)(2,1)}, u32[]{:S(2)}, u32[]{:S(2)}) collective-permute-start(bf16[1,8,512,128]{3,2,1,0:T(8,128)(2,1)} %bitcast.180), channel_id=1, source_target_pairs={{4,0},{8,4},{12,8},{16,12},{20,16},{24,20},{28,24},{32,28},{36,32}... | collective-permute-start | bytes 3145736 | tf_op jit(solution)/shard_map/ppermute | solution.py:26
  297.4 118.1 %copy-start.105 = (bf16[25]{0:T(256)(128)(2,1)S(1)}, bf16[25]{0:T(256)(128)(2,1)}, u32[]{:S(2)}) copy-start(bf16[25]{0:T(256)(128)(2,1)} %copy-done.102) | copy-start | bytes 154
  301.2 119.8 %copy-start.99 = (pred[8]{0:T(512)(128)(4,1)S(1)}, pred[8]{0:T(512)(128)(4,1)}, u32[]{:S(2)}) copy-start(pred[8]{0:T(512)(128)(4,1)} %copy-done.96) | copy-start | bytes 28
  (100 other events, 449.2 us)
Sparse Core Ops, SparseCore 0:
  298.6 111.6 all-reduce.6
where the time goes:
time: 501 us; the launch traced here: 491 us
  local copies, waits for them, and re-layouts  203 us (41%)
  waiting for transfers between devices  123 us (25%)
  matrix products  63.4 us (13%)
  other arithmetic  62.4 us (12%)
  starting transfers between devices  22.6 us (5%)
  between operations  17 us (3%)
    psum x1, waiting for transfers between devices, body(): lax.psum(grad_w1.astype(jnp.bfloat16), 'space').astype(jnp.float32)  107 us
    gather x32, local copies, waits for them, and re-layouts, assemble(): fetched = jnp.take(rim_cells, source_index[:, column], axis=0)  56.9 us
    unnamed x343, local copies, waits for them, and re-layouts  48.5 us
    dot_general x12, matrix products, convolve(): jnp.dot(stacked, weight_block.reshape(9 * channels, channels), preferred_...  43.5 us
    slice x8, local copies, waits for them, and re-layouts, window_stack(): padded[:, corner_x:corner_x + length, corner_y:corner_y + length, corner_...  42.7 us
    select_n x36, other arithmetic, assemble(): fetched = jnp.take(rim_cells, source_index[:, column], axis=0)  35.7 us
    scatter x32, local copies, waits for them, and re-layouts, assemble(): padded = padded.at[:, target_x, target_y, 1:length + 1].set(fetched)  23.1 us
    dot_general x6, matrix products, weight_grad(): lax.dot_general(stacked, grads, (((0,), (0,)), ((), ())), preferred_eleme...  19.9 us
  transfers between devices with their start and end apart: 9, of which 6 were waited for; matrix products, arithmetic and copies ran while one was open for 9% of the time, Pallas kernels for 0%

commit v1 on v0

v1 whole, which is shorter than its diff:
```python
import functools
import math

import jax
import jax.numpy as jnp
from jax import lax
from jax.experimental import pallas as pl
from jax.experimental.pallas import tpu as pltpu
from jax.sharding import PartitionSpec as P

BF = jnp.bfloat16
F32 = jnp.float32
C = 128
MESH = pl.DeviceIdType.MESH

A0, A7, B0, B7 = 0, 1, 2, 3


def shifted(v):
    row = lax.broadcasted_iota(jnp.int32, v.shape, v.ndim - 1 - 1)
    down = jnp.where(row == 0, 0.0, pltpu.roll(v, 1, v.ndim - 2))
    up = jnp.where(row == 7, 0.0, pltpu.roll(v, 7, v.ndim - 2))
    return down, v, up


def put_plane(x_ref, a, v):
    for k, s in enumerate(shifted(v.reshape(64, 8, C))):
        x_ref[:, 1 + a, 1:9, :, C * k : C * k + C] = s.reshape(4, 8, 16, C).astype(BF)


def pair_plane(ref, a):
    v = ref[:, a].astype(F32).reshape(4, 2, 8, 8, C)
    return jnp.stack([v[:, 0], v[:, 1]], axis=2).reshape(4, 8, 16, C)


def unpair_plane(ref, a, v):
    w = v.reshape(4, 8, 2, 8, C)
    for half in range(2):
        ref[:, half, a] = w[:, :, half].astype(BF)


def take_faces(x_ref, h_ref):
    def body(p, _):
        for half in range(2):
            for face, cells in (
                (A0, x_ref[p, 1, 1:9, :, C : 2 * C]),
                (A7, x_ref[p, 8, 1:9, :, C : 2 * C]),
                (B0, x_ref[p, 1:9, 1, :, C : 2 * C]),
                (B7, x_ref[p, 1:9, 8, :, C : 2 * C]),
            ):
                v = cells.astype(F32).reshape(8, 2, 8, C)
                h_ref[8 + 2 * p + half, face] = v[:, half].astype(BF)
        return 0

    lax.fori_loop(0, 4, body, 0)


def fill_rim(x_ref, h_ref, nbr_ref, first):
    def body(p, _):
        def source(column):
            out = []
            for half in range(2):
                n = nbr_ref[2 * p + half, column]
                out.append(jnp.where(n >= 0, jnp.clip(n - first, 0, 23), 24))
            return out

        def line(column, face):
            i, j = source(column)
            u = h_ref[i, face].astype(F32)
            v = h_ref[j, face].astype(F32)
            w = jnp.stack([u, v], axis=1).reshape(16, 8, C)
            return [s.reshape(8, 16, C).astype(BF) for s in shifted(w)]

        def cell(column, face, where):
            i, j = source(column)
            u = h_ref[i, face, where].astype(F32)
            v = h_ref[j, face, where].astype(F32)
            w = jnp.stack([u, v], axis=0)
            return [s.reshape(16, C).astype(BF) for s in shifted(w)]

        for column, face, where, i, j in (
            (0, A7, 7, 0, 0),
            (2, A7, 0, 0, 9),
            (5, A0, 7, 9, 0),
            (7, A0, 0, 9, 9),
        ):
            for k, s in enumerate(cell(column, face, where)):
                x_ref[p, i, j, :, C * k : C * k + C] = s
        for column, face, i in ((1, A7, 0), (6, A0, 9)):
            for k, s in enumerate(line(column, face)):
                x_ref[p, i, 1:9, :, C * k : C * k + C] = s
        for column, face, j in ((3, B7, 0), (4, B0, 9)):
            for k, s in enumerate(line(column, face)):
                x_ref[p, 1:9, j, :, C * k : C * k + C] = s
        return 0

    lax.fori_loop(0, 4, body, 0)


def build_taps(t_ref, w_ref, flipped):
    def body(t, _):
        zero = jnp.zeros((C, C), BF)
        t_ref[t, :, C:] = zero
        t_ref[27 + t, :, :C] = zero
        for k in range(3):
            if flipped:
                w = w_ref[26 - (9 * k + t)].astype(F32).T.astype(BF)
            else:
                w = w_ref[9 * k + t]
            t_ref[9 * k + t, :, :C] = w
            t_ref[9 * k + 9 + t, :, C:] = w
        return 0

    lax.fori_loop(0, 9, body, 0)


def convolve(x_ref, t_ref, epilogue, between=None):
    def body(q, _):
        windows = [
            x_ref[:, 2 * q + p, k : k + 8].reshape(512, 3 * C) for p in range(4) for k in range(3)
        ]
        total = jnp.dot(
            jnp.concatenate(windows, axis=1),
            t_ref[...].reshape(36 * C, 2 * C),
            preferred_element_type=F32,
        )
        for u in range(2):
            epilogue(2 * q + u, total[:, C * u : C * u + C].reshape(4, 8, 16, C))
        if between is not None:
            between(q)
        return 0

    lax.fori_loop(0, 4, body, 0)


def put_transposed(gt_ref, a, v):
    flat = v.reshape(4, C, C)
    for p in range(4):
        gt_ref[p // 2, a + 2, :, C * (p % 2) : C * (p % 2) + C] = flat[p].T.astype(BF)


def weight_grad(x_ref, gt_ref, g_ref, scale):
    def body(k, _):
        total = None
        for i in range(0, 10, 2):
            left = jnp.concatenate(
                [gt_ref[h, i + q : i + q + 3].reshape(384, 256) for q in range(2) for h in range(2)],
                axis=1,
            )
            right = jnp.concatenate(
                [x_ref[:, i + q, pl.ds(k, 8)].reshape(512, 384) for q in range(2)], axis=0
            )
            d = jnp.dot(left, right, preferred_element_type=F32)
            total = d if total is None else total + d
        total = total * scale
        for q in range(3):
            for z in range(3):
                block = total[C * q : C * q + C, C * z : C * z + C].T.astype(BF)
                tap = 9 * (2 - q) + 3 * k + z
                for s in range(8):
                    g_ref[s % 2, s // 2, tap] = block[16 * s : 16 * s + 16]
        return 0

    lax.fori_loop(0, 3, body, 0)


class Reduction:
    def __init__(self, place, refs):
        self.place = place
        (self.g, self.r0, self.s0, self.r1, self.s1, self.r2, self.fin, self.send, self.recv) = refs
        self.started = []

    def copy(self, src, dst, slot, peer):
        return pltpu.make_async_remote_copy(
            src_ref=src,
            dst_ref=dst,
            send_sem=self.send.at[slot],
            recv_sem=self.recv.at[slot],
            device_id={"space": peer},
            device_id_type=MESH,
        )

    def phase(self, n):
        p = self.place
        core, ma, mb = p["core"], p["ma"], p["mb"]
        if n == 0:
            return [self.copy(self.g.at[1 - core], self.r0, 0, p["sibling"])]
        if n == 5:
            return [self.copy(self.fin.at[core], self.fin.at[core], 13, p["sibling"])]
        copies = []
        for d in range(3):
            pa, pb = p["peers_a"][d], p["peers_b"][d]
            if n == 1:
                copies.append(self.copy(self.s0.at[pa[0]], self.r1.at[d], 1 + d, pa[1]))
            elif n == 2:
                copies.append(
                    self.copy(self.s1.at[pl.ds(7 * pb[0], 7)], self.r2.at[d], 4 + d, pb[1])
                )
            elif n == 3:
                mine = self.fin.at[core, ma, pl.ds(7 * mb, 7)]
                copies.append(self.copy(mine, mine, 7 + d, pb[1]))
            else:
                mine = self.fin.at[core, ma]
                copies.append(self.copy(mine, mine, 10 + d, pa[1]))
        return copies

    def start(self, n):
        for c in self.phase(n):
            c.start()

    def wait(self, n):
        for c in self.phase(n):
            c.wait_recv()

    def drain(self):
        for n in range(6):
            for c in self.phase(n):
                c.wait_send()

    def step(self, n):
        p = self.place
        core, ma, mb = p["core"], p["ma"], p["mb"]
        if n == 0:
            self.start(0)
            return
        self.wait(n - 1)
        if n == 1:

            def add(i, _):
                self.s0[i] = (self.g[core, i].astype(F32) + self.r0[i].astype(F32)).astype(BF)
                return 0

            lax.fori_loop(0, 4, add, 0)
        elif n == 2:
            v = self.s0[ma].astype(F32)
            for d in range(3):
                v = v + self.r1[d].astype(F32)
            self.s1[...] = v.astype(BF)
        elif n == 3:
            v = self.s1[pl.ds(7 * mb, 7)].astype(F32)
            for d in range(3):
                v = v + self.r2[d].astype(F32)
            self.fin[core, ma, pl.ds(7 * mb, 7)] = v.astype(BF)
        if n < 6:
            self.start(n)


def silu_parts(v):
    s = 1.0 / (1.0 + jnp.exp(-v))
    return s, s * (1.0 + v * (1.0 - s))


def kernel(
    scale,
    feats_h, mask_h, nbr_ref, w1_h, w2_h, cot_h,
    out_h, gin_h, gw1_h, gw2_h,
    feats, mask, w1, w2, cot, out_s,
    xin, xhid, xg, taps, maskb, pre1, gt,
    h0, h1, h2, h3,
    load_sem, store_sem, face_send, face_recv,
    *red_refs,
):
    me = lax.axis_index("space")
    n_space = 32
    core = lax.rem(me, 2)
    chip = me // 2
    z = lax.rem(chip, 4)
    y = chip // 4
    right, left = lax.rem(me + 1, n_space), lax.rem(me + n_space - 1, n_space)
    ma = (1 - core) * y + core * z
    mb = (1 - core) * z + core * y
    sa = 8 - 6 * core
    sb = 2 + 6 * core
    peers_a, peers_b = [], []
    for d in range(1, 4):
        ca, cb = lax.rem(ma + d, 4), lax.rem(mb + d, 4)
        peers_a.append((ca, me + (ca - ma) * sa))
        peers_b.append((cb, me + (cb - mb) * sb))
    place = {
        "core": core, "ma": ma, "mb": mb, "sibling": me + 1 - 2 * core,
        "peers_a": peers_a, "peers_b": peers_b,
    }
    first = 8 * (me - 1)
    red2 = Reduction(place, red_refs[:9])
    red1 = Reduction(place, red_refs[9:])

    loads = [
        pltpu.make_async_copy(src, dst, load_sem.at[i])
        for i, (src, dst) in enumerate(
            ((feats_h, feats), (mask_h, mask), (w1_h, w1), (w2_h, w2), (cot_h, cot))
        )
    ]
    for c in loads:
        c.start()

    barrier = pltpu.get_barrier_semaphore()
    for peer in [left, right] + [q for _, q in peers_a] + [q for _, q in peers_b]:
        pl.semaphore_signal(barrier, inc=1, device_id={"space": peer}, device_id_type=MESH)
    pl.semaphore_wait(barrier, 8)

    faces = (h0, h1, h2, h3)

    def face_copies(n):
        h = faces[n]
        return [
            pltpu.make_async_remote_copy(
                src_ref=h.at[pl.ds(8, 8)],
                dst_ref=h.at[pl.ds(at, 8)],
                send_sem=face_send.at[n, side],
                recv_sem=face_recv.at[n, side],
                device_id={"space": peer},
                device_id_type=MESH,
            )
            for side, (at, peer) in enumerate(((0, right), (16, left)))
        ]

    def send_faces(n, x_ref):
        take_faces(x_ref, faces[n])
        for c in face_copies(n):
            c.start()

    def receive_faces(n, x_ref):
        for c in face_copies(n):
            c.wait_recv()
        fill_rim(x_ref, faces[n], nbr_ref, first)

    for h in faces:
        h[24] = jnp.zeros((4, 8, 8, C), BF)
    for red in (red1, red2):
        for side in range(2):
            for q in range(4):
                red.g[side, q, 27] = jnp.zeros((16, C), BF)
    for side in range(2):
        for a in (0, 1, 10, 11):
            gt[side, a] = jnp.zeros((C, 2 * C), BF)

    loads[1].wait()
    loads[0].wait()

    def mask_plane(a, _):
        row = lax.broadcasted_iota(jnp.int32, (C, C), 0)
        lane = lax.broadcasted_iota(jnp.int32, (C, C), 1)
        hit = lane == lax.rem(a, 2) * 64 + (row // 16) * 8 + lax.rem(row, 8)
        second = lax.rem(row // 8, 2) == 1
        at = pl.ds(pl.multiple_of((a // 2) * C, C), C)
        pieces = []
        for p in range(4):
            m0 = mask[2 * p : 2 * p + 1, at].astype(F32)
            m1 = mask[2 * p + 1 : 2 * p + 2, at].astype(F32)
            pieces.append(jnp.where(hit, jnp.where(second, m1, m0), 0.0).astype(BF))
        spread = jnp.dot(
            jnp.concatenate(pieces, axis=0), jnp.ones((C, C), BF), preferred_element_type=F32
        )
        m = spread.reshape(4, 8, 16, C)
        maskb[a] = m.astype(BF)
        put_plane(xin, a, pair_plane(feats, a) * m)
        return 0

    lax.fori_loop(0, 8, mask_plane, 0)
    send_faces(0, xin)

    loads[2].wait()
    loads[3].wait()
    build_taps(taps.at[0], w1, False)
    build_taps(taps.at[2], w2, True)
    receive_faces(0, xin)

    def first_done(a, v):
        pre1[a] = v
        s, _ = silu_parts(v)
        put_plane(xhid, a, maskb[a].astype(F32) * (v * s))

    convolve(xin, taps.at[0], first_done)
    send_faces(1, xhid)
    build_taps(taps.at[1], w2, False)
    build_taps(taps.at[3], w1, True)
    loads[4].wait()
    receive_faces(1, xhid)

    def second_done(a, v):
        s, slope = silu_parts(v)
        m = maskb[a].astype(F32)
        unpair_plane(out_s, a, m * (v * s))
        g = pair_plane(cot, a) * m * slope
        put_plane(xg, a, g)
        put_transposed(gt, a, g)

    convolve(xhid, taps.at[1], second_done)
    send_faces(2, xg)
    store_out = pltpu.make_async_copy(out_s, out_h, store_sem.at[0])
    store_out.start()

    weight_grad(xhid, gt, red2.g, scale)
    red2.step(0)
    receive_faces(2, xg)

    def third_done(a, v):
        _, slope = silu_parts(pre1[a])
        g = maskb[a].astype(F32) * slope * v
        put_plane(xhid, a, g)
        put_transposed(gt, a, g)

    convolve(xg, taps.at[2], third_done)
    send_faces(3, xhid)
    red2.step(1)
    store_out.wait()

    weight_grad(xin, gt, red1.g, scale)
    red1.step(0)
    red2.step(2)
    receive_faces(3, xhid)
    red1.step(1)

    def last_done(a, v):
        unpair_plane(out_s, a, maskb[a].astype(F32) * v)

    def between(q):
        for n in range(4):

            @pl.when(q == n)
            def _():
                if n < 3:
                    red2.step(3 + n)
                if n > 0:
                    red1.step(1 + n)

    convolve(xhid, taps.at[3], last_done, between)
    store_gin = pltpu.make_async_copy(out_s, gin_h, store_sem.at[1])
    store_gin.start()
    red2.step(6)
    store_w2 = pltpu.make_async_copy(red2.fin, gw2_h, store_sem.at[2])
    store_w2.start()
    for n in (5, 6):
        red1.step(n)
    store_w1 = pltpu.make_async_copy(red1.fin, gw1_h, store_sem.at[3])
    store_w1.start()
    for n in range(4):
        for c in face_copies(n):
            c.wait_send()
    red1.drain()
    red2.drain()
    store_gin.wait()
    store_w2.wait()
    store_w1.wait()


def body(feats, mask, neighbours, weight_one, weight_two, cotangent):
    bricks, voxels, channels = feats.shape
    scale = 1.0 / math.sqrt(voxels * bricks)
    cube = (bricks, 8, 8, 8, channels)
    field = pltpu.VMEM((4, 10, 10, 16, 3 * C), BF)
    face_buffer = pltpu.VMEM((25, 4, 8, 8, C), BF)
    reduction = [
        pltpu.VMEM((2, 4, 28, 16, C), BF),
        pltpu.VMEM((4, 28, 16, C), BF),
        pltpu.VMEM((4, 28, 16, C), BF),
        pltpu.VMEM((3, 28, 16, C), BF),
        pltpu.VMEM((28, 16, C), BF),
        pltpu.VMEM((3, 7, 16, C), BF),
        pltpu.VMEM((2, 4, 28, 16, C), BF),
        pltpu.SemaphoreType.DMA((14,)),
        pltpu.SemaphoreType.DMA((14,)),
    ]
    anywhere = pl.BlockSpec(memory_space=pl.ANY)
    out, gin, gw1, gw2 = pl.pallas_call(
        functools.partial(kernel, scale),
        out_shape=(
            jax.ShapeDtypeStruct((4, 2, 8, 8, 8, C), BF),
            jax.ShapeDtypeStruct((4, 2, 8, 8, 8, C), BF),
            jax.ShapeDtypeStruct((2, 4, 28, 16, C), BF),
            jax.ShapeDtypeStruct((2, 4, 28, 16, C), BF),
        ),
        in_specs=[
            anywhere, anywhere, pl.BlockSpec(memory_space=pltpu.SMEM), anywhere, anywhere, anywhere,
        ],
        out_specs=(anywhere,) * 4,
        scratch_shapes=[
            pltpu.VMEM(cube, BF),
            pltpu.VMEM((bricks, voxels), jnp.int32),
            pltpu.VMEM((27, C, C), BF),
            pltpu.VMEM((27, C, C), BF),
            pltpu.VMEM(cube, BF),
            pltpu.VMEM((4, 2, 8, 8, 8, C), BF),
            field, field, field,
            pltpu.VMEM((4, 36, C, 2 * C), BF),
            pltpu.VMEM((8, 4, 8, 16, C), BF),
            pltpu.VMEM((8, 4, 8, 16, C), F32),
            pltpu.VMEM((2, 12, C, 2 * C), BF),
            face_buffer, face_buffer, face_buffer, face_buffer,
            pltpu.SemaphoreType.DMA((5,)),
            pltpu.SemaphoreType.DMA((4,)),
            pltpu.SemaphoreType.DMA((4, 2)),
            pltpu.SemaphoreType.DMA((4, 2)),
            *reduction,
            *reduction,
        ],
        compiler_params=pltpu.CompilerParams(
            collective_id=0, has_side_effects=True, vmem_limit_bytes=60 * 2**20
        ),
        name="bricks",
    )(feats.reshape(cube), mask, neighbours, weight_one, weight_two, cotangent.reshape(cube))

    def unfold(g):
        g = g[:, :, :27].transpose(2, 1, 0, 3, 4)
        return g.reshape(27, C, C).astype(F32)

    return (
        out.reshape(bricks, voxels, channels),
        gin.reshape(bricks, voxels, channels),
        unfold(gw1),
        unfold(gw2),
    )


def solution(mesh):
    in_specs = (
        P(("scene", "space"), None, None),
        P(("scene", "space"), None),
        P(("scene", "space"), None),
        P(),
        P(),
        P(("scene", "space"), None, None),
    )
    out_specs = (
        P(("scene", "space"), None, None),
        P(("scene", "space"), None, None),
        P("scene", None, None),
        P("scene", None, None),
    )
    return jax.shard_map(body, mesh=mesh, in_specs=in_specs, out_specs=out_specs, check_vma=False)
```

time: 501 us -> 105 us (0.21); the launches traced: 491 us -> 104 us
  local copies, waits for them, and re-layouts: 203 us -> 5.53 us
  waiting for transfers between devices: 123 us -> 0 us
  Pallas kernels: 0 us -> 96.5 us
  matrix products: 63.4 us -> 0 us
  other arithmetic: 62.4 us -> 1.75 us
  starting transfers between devices: 22.6 us -> 0 us
  between operations: 17 us -> 0.65 us
    psum x1 -> x0, waiting for transfers between devices: 107 us -> none  [body(): lax.psum(grad_w1.astype(jnp.bfloat16), 'space').astype(jnp.float32)]
    pallas_call x0 -> x1, Pallas kernels: none -> 96.5 us  [body(): pl.pallas_call(functools.partial(kernel, scale), out_shape=(jax.ShapeDtyp...]
    dot_general x18 -> x0, matrix products: 63.4 us -> none  [the longest x12 43.5 us: convolve(): jnp.dot(stacked, weight_block.reshape(9 * channels, channels), preferred_...]
    gather x32 -> x0, local copies, waits for them, and re-layouts: 56.9 us -> none  [assemble(): fetched = jnp.take(rim_cells, source_index[:, column], axis=0)]
    unnamed x343 -> x6, local copies, waits for them, and re-layouts: 48.5 us -> 2.57 us
    slice x9 -> x0, local copies, waits for them, and re-layouts: 43 us -> none  [the longest x8 42.7 us: window_stack(): padded[:, corner_x:corner_x + length, corner_y:corner_y + length, corner_...]
    select_n x37 -> x0, other arithmetic: 36.4 us -> none  [the longest x36 35.7 us: assemble(): fetched = jnp.take(rim_cells, source_index[:, column], axis=0)]
    scatter x32 -> x0, local copies, waits for them, and re-layouts: 23.1 us -> none  [assemble(): padded = padded.at[:, target_x, target_y, 1:length + 1].set(fetched)]
  transfers between devices with their start and end apart: 9 -> 0, of which waited for: 6 -> 0; matrix products, arithmetic and copies ran while one was open for 9% -> 0% of each run, Pallas kernels for 0% -> 0%
where the time goes in v1:
time: 105 us; the launch traced here: 104 us
  Pallas kernels  96.5 us (92%)
  local copies, waits for them, and re-layouts  5.53 us (5%)
  other arithmetic  1.75 us (2%)
    pallas_call x1, Pallas kernels, body(): pl.pallas_call(functools.partial(kernel, scale), out_shape=(jax.ShapeDtyp...  96.5 us
    convert_element_type x2, local copies, waits for them, and re-layouts, unfold(): return g.reshape(27, C, C).astype(F32)  2.95 us
    unnamed x6, local copies, waits for them, and re-layouts  2.57 us

profile of v1, /device:TPU:1, one launch (start us, length us, event | category | flops | bytes accessed | tf_op | source)
XLA Modules:
  0.0 104.4 jit_solution(17386009970652067588)
XLA Ops:
  0.6 96.5 %bricks.1 = (bf16[4,2,8,8,8,128]{5,4,3,2,1,0:T(8,128)(2,1)}, bf16[4,2,8,8,8,128]{5,4,3,2,1,0:T(8,128)(2,1)}, bf16[2,4,28,16,128]{4,3,2,1,0:T(8,128)(2,1)}, bf16[2,4,28,16,128]{4,3,2,1,0:T(8,128)(2,1)}) custom-call(bf16[8,8,8,8,128]{4,3,2,1,0:T(8,128)(2,1)} %bitcast.12, s32[8,512]{1,0:T(8,128)} %mask_h.1, s32[8,8]{1,0:T(8,128)} %nbr_ref.1, ...), custom_call_target="tpu_custom_call" | custom-call | tf_op jit(solution)/shard_map/bricks/pallas_call | solution.py:465
  97.2 1.8 %convert_bitcast_fusion = (f32[27,4,2,16,128]{4,3,0,1,2:T(8,128)S(1)}, f32[27,4,2,16,128]{4,3,0,1,2:T(8,128)S(1)}) fusion(bf16[2,4,28,16,128]{4,3,2,1,0:T(8,128)(2,1)} %get-tuple-element.11, bf16[2,4,28,16,128]{4,3,2,1,0:T(8,128)(2,1)} %get-tuple-element.10), kind=kLoop, calls=%fused_computation | loop fusion | flops 884736 | bytes 5308416 | tf_op jit(solution)/shard_map/convert_element_type | solution.py:505
  98.9 1.5 %copy.11 = f32[27,4,2,16,128]{4,3,2,1,0:T(8,128)} copy(f32[27,4,2,16,128]{4,3,0,1,2:T(8,128)S(1)} %get-tuple-element.12) | data formatting | bytes 3538944 | tf_op jit(solution)/shard_map/convert_element_type | solution.py:505
  100.4 0.0 copy-start.1
  100.4 1.5 %copy.10 = f32[27,4,2,16,128]{4,3,2,1,0:T(8,128)} copy(f32[27,4,2,16,128]{4,3,0,1,2:T(8,128)S(1)} %get-tuple-element.13) | data formatting | bytes 3538944 | tf_op jit(solution)/shard_map/convert_element_type | solution.py:505
  101.9 0.0 copy-start
  101.9 0.0 copy-done.1
  101.9 1.0 copy.14
  102.8 0.6 copy-done
  103.5 1.0 copy.15
Async XLA Ops:
  100.4 1.5 %copy-start.1 = (bf16[4,2,8,8,8,128]{5,4,3,2,1,0:T(8,128)(2,1)S(1)}, bf16[4,2,8,8,8,128]{5,4,3,2,1,0:T(8,128)(2,1)}, u32[]{:S(2)}) copy-start(bf16[4,2,8,8,8,128]{5,4,3,2,1,0:T(8,128)(2,1)} %get-tuple-element.8) | copy-start | bytes 3145732
  101.9 1.6 %copy-start = (bf16[4,2,8,8,8,128]{5,4,3,2,1,0:T(8,128)(2,1)S(1)}, bf16[4,2,8,8,8,128]{5,4,3,2,1,0:T(8,128)(2,1)}, u32[]{:S(2)}) copy-start(bf16[4,2,8,8,8,128]{5,4,3,2,1,0:T(8,128)(2,1)} %get-tuple-element.9) | copy-start | bytes 3145732

commit v2 on v1

--- a/solution.py
+++ b/solution.py
@@ -139,36 +139,75 @@
         gt_ref[p // 2, a + 2, :, C * (p % 2) : C * (p % 2) + C] = flat[p].T.astype(BF)
 
 
-def weight_grad(x_ref, gt_ref, g_ref, scale):
-    def body(k, _):
-        total = None
-        for i in range(0, 10, 2):
-            left = jnp.concatenate(
-                [gt_ref[h, i + q : i + q + 3].reshape(384, 256) for q in range(2) for h in range(2)],
-                axis=1,
-            )
-            right = jnp.concatenate(
-                [x_ref[:, i + q, pl.ds(k, 8)].reshape(512, 384) for q in range(2)], axis=0
-            )
-            d = jnp.dot(left, right, preferred_element_type=F32)
-            total = d if total is None else total + d
-        total = total * scale
-        for q in range(3):
-            for z in range(3):
-                block = total[C * q : C * q + C, C * z : C * z + C].T.astype(BF)
-                tap = 9 * (2 - q) + 3 * k + z
-                for s in range(8):
-                    g_ref[s % 2, s // 2, tap] = block[16 * s : 16 * s + 16]
-        return 0
-
-    lax.fori_loop(0, 3, body, 0)
+def weight_grad(x_ref, gt_ref, columns, scale, store):
+    totals = [None] * 3
+    for i in range(0, 10, 2):
+        low, high = (1 if i == 0 else 0), (2 if i == 8 else 3)
+        left = jnp.concatenate(
+            [
+                gt_ref[h, i + q + low : i + q + high].reshape(C * (high - low), 2 * C)
+                for q in range(2)
+                for h in range(2)
+            ],
+            axis=1,
+        )
+        right = jnp.concatenate(
+            [
+                jnp.concatenate(
+                    [
+                        x_ref[:, i + q, c // 3 : c // 3 + 8, :, C * (c % 3) : C * (c % 3) + C]
+                        .reshape(512, C)
+                        for c in columns
+                    ],
+                    axis=1,
+                )
+                for q in range(2)
+            ],
+            axis=0,
+        )
+        d = jnp.dot(left, right, preferred_element_type=F32)
+        for q in range(low, high):
+            part = d[C * (q - low) : C * (q - low) + C]
+            totals[q] = part if totals[q] is None else totals[q] + part
+    for q in range(3):
+        for n, c in enumerate(columns):
+            store(q, c, (totals[q][:, C * n : C * n + C] * scale).T)
+
+
+LEFT_COLUMNS, RIGHT_COLUMNS = range(4), range(4, 9)
+
+
+def slots_of(taps):
+    return (taps + 1) // 2
 
 
 class Reduction:
-    def __init__(self, place, refs):
+    def __init__(self, place, taps, refs):
         self.place = place
-        (self.g, self.r0, self.s0, self.r1, self.s1, self.r2, self.fin, self.send, self.recv) = refs
-        self.started = []
+        self.taps = taps
+        self.g, self.r0, self.s0, self.r1, self.fin, self.send, self.recv = refs
+
+    @staticmethod
+    def scratch(taps):
+        n = slots_of(taps)
+        return [
+            pltpu.VMEM((2, 16, n, 8, C), BF),
+            pltpu.VMEM((16, n, 8, C), BF),
+            pltpu.VMEM((16, n, 8, C), BF),
+            pltpu.VMEM((15, n, 8, C), BF),
+            pltpu.VMEM((2, 16, n, 8, C), BF),
+            pltpu.SemaphoreType.DMA((47,)),
+            pltpu.SemaphoreType.DMA((47,)),
+        ]
+
+    def clear(self):
+        if self.taps % 2:
+            self.g[:, 8:, slots_of(self.taps) - 1] = jnp.zeros((2, 8, 8, C), BF)
+
+    def put(self, tap, block):
+        for u in range(16):
+            n = 8 * tap + u // 2
+            self.g[u % 2, n % 16, n // 16] = block[8 * u : 8 * u + 8].astype(BF)
 
     def copy(self, src, dst, slot, peer):
         return pltpu.make_async_remote_copy(
@@ -180,69 +219,76 @@
             device_id_type=MESH,
         )
 
-    def phase(self, n):
-        p = self.place
-        core, ma, mb = p["core"], p["ma"], p["mb"]
+    def pair(self):
+        return self.copy(self.g.at[1 - self.place["core"]], self.r0, 0, self.place["sibling"])
+
+    def scatter(self, d):
+        chip = self.place["chip"](d)
+        return self.copy(
+            self.s0.at[chip], self.r1.at[d - 1], d, 2 * chip + self.place["core"]
+        )
+
+    def gather(self, d):
+        mine = self.fin.at[self.place["core"], self.place["chip"](0)]
+        return self.copy(mine, mine, 15 + d, 2 * self.place["chip"](d) + self.place["core"])
+
+    def forward(self, d):
+        one = self.fin.at[self.place["core"], self.place["behind"](d)]
+        return self.copy(one, one, 31 + d, self.place["sibling"])
+
+    def step(self, n):
+        core, chip = self.place["core"], self.place["chip"]
+
+        def each(low, run):
+            def body(d, _):
+                run(d)
+                return 0
+
+            lax.fori_loop(low, 16, body, 0)
+
         if n == 0:
-            return [self.copy(self.g.at[1 - core], self.r0, 0, p["sibling"])]
-        if n == 5:
-            return [self.copy(self.fin.at[core], self.fin.at[core], 13, p["sibling"])]
-        copies = []
-        for d in range(3):
-            pa, pb = p["peers_a"][d], p["peers_b"][d]
-            if n == 1:
-                copies.append(self.copy(self.s0.at[pa[0]], self.r1.at[d], 1 + d, pa[1]))
-            elif n == 2:
-                copies.append(
-                    self.copy(self.s1.at[pl.ds(7 * pb[0], 7)], self.r2.at[d], 4 + d, pb[1])
-                )
-            elif n == 3:
-                mine = self.fin.at[core, ma, pl.ds(7 * mb, 7)]
-                copies.append(self.copy(mine, mine, 7 + d, pb[1]))
-            else:
-                mine = self.fin.at[core, ma]
-                copies.append(self.copy(mine, mine, 10 + d, pa[1]))
-        return copies
-
-    def start(self, n):
-        for c in self.phase(n):
-            c.start()
-
-    def wait(self, n):
-        for c in self.phase(n):
-            c.wait_recv()
+            self.pair().start()
+        elif n == 1:
+            self.pair().wait_recv()
+
+            def add(c):
+                self.s0[c] = (self.g[core, c].astype(F32) + self.r0[c].astype(F32)).astype(BF)
+
+            def send(d):
+                add(chip(d))
+                self.scatter(d).start()
+
+            each(1, send)
+            add(chip(0))
+        elif n == 2:
+            each(1, lambda d: self.scatter(d).wait_recv())
+            v = self.s0[chip(0)].astype(F32)
+            for d in range(15):
+                v = v + self.r1[d].astype(F32)
+            self.fin[core, chip(0)] = v.astype(BF)
+            each(1, lambda d: self.gather(d).start())
+            self.forward(0).start()
+        elif n == 3:
+
+            def pass_on(d):
+                self.gather(d).wait_recv()
+                self.forward(d).start()
+
+            each(1, pass_on)
+        else:
+            each(0, lambda d: self.forward(d).wait_recv())
 
     def drain(self):
-        for n in range(6):
-            for c in self.phase(n):
-                c.wait_send()
-
-    def step(self, n):
-        p = self.place
-        core, ma, mb = p["core"], p["ma"], p["mb"]
-        if n == 0:
-            self.start(0)
-            return
-        self.wait(n - 1)
-        if n == 1:
-
-            def add(i, _):
-                self.s0[i] = (self.g[core, i].astype(F32) + self.r0[i].astype(F32)).astype(BF)
-                return 0
-
-            lax.fori_loop(0, 4, add, 0)
-        elif n == 2:
-            v = self.s0[ma].astype(F32)
-            for d in range(3):
-                v = v + self.r1[d].astype(F32)
-            self.s1[...] = v.astype(BF)
-        elif n == 3:
-            v = self.s1[pl.ds(7 * mb, 7)].astype(F32)
-            for d in range(3):
-                v = v + self.r2[d].astype(F32)
-            self.fin[core, ma, pl.ds(7 * mb, 7)] = v.astype(BF)
-        if n < 6:
-            self.start(n)
+        self.pair().wait_send()
+
+        def body(d, _):
+            self.scatter(d).wait_send()
+            self.gather(d).wait_send()
+            self.forward(d).wait_send()
+            return 0
+
+        self.forward(0).wait_send()
+        lax.fori_loop(1, 16, body, 0)
 
 
 def silu_parts(v):
@@ -253,7 +299,7 @@
 def kernel(
     scale,
     feats_h, mask_h, nbr_ref, w1_h, w2_h, cot_h,
-    out_h, gin_h, gw1_h, gw2_h,
+    out_h, gin_h, gw2_h, gw1a_h, gw1b_h,
     feats, mask, w1, w2, cot, out_s,
     xin, xhid, xg, taps, maskb, pre1, gt,
     h0, h1, h2, h3,
@@ -267,22 +313,18 @@
     z = lax.rem(chip, 4)
     y = chip // 4
     right, left = lax.rem(me + 1, n_space), lax.rem(me + n_space - 1, n_space)
-    ma = (1 - core) * y + core * z
-    mb = (1 - core) * z + core * y
-    sa = 8 - 6 * core
-    sb = 2 + 6 * core
-    peers_a, peers_b = [], []
-    for d in range(1, 4):
-        ca, cb = lax.rem(ma + d, 4), lax.rem(mb + d, 4)
-        peers_a.append((ca, me + (ca - ma) * sa))
-        peers_b.append((cb, me + (cb - mb) * sb))
-    place = {
-        "core": core, "ma": ma, "mb": mb, "sibling": me + 1 - 2 * core,
-        "peers_a": peers_a, "peers_b": peers_b,
-    }
+
+    def chip_at(d):
+        return 4 * lax.rem(y + d // 4, 4) + lax.rem(z + lax.rem(d, 4), 4)
+
+    def behind(d):
+        return 4 * lax.rem(y + 4 - d // 4, 4) + lax.rem(z + 4 - lax.rem(d, 4), 4)
+
+    place = {"core": core, "sibling": me + 1 - 2 * core, "chip": chip_at, "behind": behind}
     first = 8 * (me - 1)
-    red2 = Reduction(place, red_refs[:9])
-    red1 = Reduction(place, red_refs[9:])
+    red2 = Reduction(place, 27, red_refs[:7])
+    red1a = Reduction(place, 12, red_refs[7:14])
+    red1b = Reduction(place, 15, red_refs[14:])
 
     loads = [
         pltpu.make_async_copy(src, dst, load_sem.at[i])
@@ -294,9 +336,16 @@
         c.start()
 
     barrier = pltpu.get_barrier_semaphore()
-    for peer in [left, right] + [q for _, q in peers_a] + [q for _, q in peers_b]:
+    for peer in (left, right):
         pl.semaphore_signal(barrier, inc=1, device_id={"space": peer}, device_id_type=MESH)
-    pl.semaphore_wait(barrier, 8)
+
+    def greet(d, _):
+        peer = 2 * chip_at(d) + core
+        pl.semaphore_signal(barrier, inc=1, device_id={"space": peer}, device_id_type=MESH)
+        return 0
+
+    lax.fori_loop(1, 16, greet, 0)
+    pl.semaphore_wait(barrier, 17)
 
     faces = (h0, h1, h2, h3)
 
@@ -326,10 +375,8 @@
 
     for h in faces:
         h[24] = jnp.zeros((4, 8, 8, C), BF)
-    for red in (red1, red2):
-        for side in range(2):
-            for q in range(4):
-                red.g[side, q, 27] = jnp.zeros((16, C), BF)
+    for red in (red2, red1a, red1b):
+        red.clear()
     for side in range(2):
         for a in (0, 1, 10, 11):
             gt[side, a] = jnp.zeros((C, 2 * C), BF)
@@ -390,7 +437,11 @@
     store_out = pltpu.make_async_copy(out_s, out_h, store_sem.at[0])
     store_out.start()
 
-    weight_grad(xhid, gt, red2.g, scale)
+    def put_w2(q, c, block):
+        red2.put(9 * (2 - q) + c, block)
+
+    weight_grad(xhid, gt, LEFT_COLUMNS, scale, put_w2)
+    weight_grad(xhid, gt, RIGHT_COLUMNS, scale, put_w2)
     red2.step(0)
     receive_faces(2, xg)
 
@@ -400,48 +451,99 @@
         put_plane(xhid, a, g)
         put_transposed(gt, a, g)
 
-    convolve(xg, taps.at[2], third_done)
+    def third_between(q):
+        @pl.when(q == 0)
+        def _():
+            red2.step(1)
+
+    convolve(xg, taps.at[2], third_done, third_between)
     send_faces(3, xhid)
-    red2.step(1)
+    red2.step(2)
     store_out.wait()
 
-    weight_grad(xin, gt, red1.g, scale)
-    red1.step(0)
-    red2.step(2)
+    weight_grad(xin, gt, LEFT_COLUMNS, scale, lambda q, c, v: red1a.put(4 * (2 - q) + c, v))
+    red1a.step(0)
+    weight_grad(xin, gt, RIGHT_COLUMNS, scale, lambda q, c, v: red1b.put(5 * (2 - q) + c - 4, v))
+    red1b.step(0)
+    red1a.step(1)
+    red2.step(3)
     receive_faces(3, xhid)
-    red1.step(1)
+    red1b.step(1)
 
     def last_done(a, v):
         unpair_plane(out_s, a, maskb[a].astype(F32) * v)
 
-    def between(q):
-        for n in range(4):
-
-            @pl.when(q == n)
-            def _():
-                if n < 3:
-                    red2.step(3 + n)
-                if n > 0:
-                    red1.step(1 + n)
-
-    convolve(xhid, taps.at[3], last_done, between)
-    store_gin = pltpu.make_async_copy(out_s, gin_h, store_sem.at[1])
-    store_gin.start()
-    red2.step(6)
-    store_w2 = pltpu.make_async_copy(red2.fin, gw2_h, store_sem.at[2])
-    store_w2.start()
-    for n in (5, 6):
-        red1.step(n)
-    store_w1 = pltpu.make_async_copy(red1.fin, gw1_h, store_sem.at[3])
-    store_w1.start()
+    def last_between(q):
+        @pl.when(q == 1)
+        def _():
+            red1a.step(2)
+
+        @pl.when(q == 2)
+        def _():
+            red1b.step(2)
+
+        @pl.when(q == 3)
+        def _():
+            red2.step(4)
+            red1a.step(3)
+
+    convolve(xhid, taps.at[3], last_done, last_between)
+    stores = [
+        pltpu.make_async_copy(src, dst, store_sem.at[1 + i])
+        for i, (src, dst) in enumerate(
+            ((out_s, gin_h), (red2.fin, gw2_h), (red1a.fin, gw1a_h), (red1b.fin, gw1b_h))
+        )
+    ]
+    stores[0].start()
+    stores[1].start()
+    red1b.step(3)
+    red1a.step(4)
+    stores[2].start()
+    red1b.step(4)
+    stores[3].start()
     for n in range(4):
         for c in face_copies(n):
             c.wait_send()
-    red1.drain()
-    red2.drain()
-    store_gin.wait()
-    store_w2.wait()
-    store_w1.wait()
+    for red in (red2, red1a, red1b):
+        red.drain()
+    for c in stores:
+        c.wait()
+
+
+def finish(
+    out_t, gin_t, gw2_t, gw1a_t, gw1b_t,
+    out_h, gin_h, gw1_h, gw2_h,
+    fin2, fin1a, fin1b, w1, w2, sem,
+):
+    copies = [
+        pltpu.make_async_copy(src, dst, sem.at[i])
+        for i, (src, dst) in enumerate(
+            ((gw2_t, fin2), (gw1a_t, fin1a), (gw1b_t, fin1b), (out_t, out_h), (gin_t, gin_h),
+             (w2, gw2_h), (w1, gw1_h))
+        )
+    ]
+    for c in copies[:5]:
+        c.start()
+
+    def order(fin, tap, dst, to):
+        for u in range(16):
+            n = 8 * tap + u // 2
+            dst[to, 8 * u : 8 * u + 8] = fin[u % 2, n % 16, n // 16].astype(F32)
+
+    copies[0].wait()
+    for tap in range(27):
+        order(fin2, tap, w2, tap)
+    copies[5].start()
+    copies[1].wait()
+    copies[2].wait()
+    for k in range(3):
+        for c in LEFT_COLUMNS:
+            order(fin1a, 4 * k + c, w1, 9 * k + c)
+        for c in RIGHT_COLUMNS:
+            order(fin1b, 5 * k + c - 4, w1, 9 * k + c)
+    copies[6].start()
+    for c in copies[3:]:
+        c.wait()
 
 
 def body(feats, mask, neighbours, weight_one, weight_two, cotangent):
@@ -450,30 +552,19 @@
     cube = (bricks, 8, 8, 8, channels)
     field = pltpu.VMEM((4, 10, 10, 16, 3 * C), BF)
     face_buffer = pltpu.VMEM((25, 4, 8, 8, C), BF)
-    reduction = [
-        pltpu.VMEM((2, 4, 28, 16, C), BF),
-        pltpu.VMEM((4, 28, 16, C), BF),
-        pltpu.VMEM((4, 28, 16, C), BF),
-        pltpu.VMEM((3, 28, 16, C), BF),
-        pltpu.VMEM((28, 16, C), BF),
-        pltpu.VMEM((3, 7, 16, C), BF),
-        pltpu.VMEM((2, 4, 28, 16, C), BF),
-        pltpu.SemaphoreType.DMA((14,)),
-        pltpu.SemaphoreType.DMA((14,)),
+    anywhere = pl.BlockSpec(memory_space=pl.ANY)
+    parts = [
+        jax.ShapeDtypeStruct((4, 2, 8, 8, 8, C), BF),
+        jax.ShapeDtypeStruct((4, 2, 8, 8, 8, C), BF),
+        *(jax.ShapeDtypeStruct((2, 16, slots_of(n), 8, C), BF) for n in (27, 12, 15)),
     ]
-    anywhere = pl.BlockSpec(memory_space=pl.ANY)
-    out, gin, gw1, gw2 = pl.pallas_call(
+    left_over = pl.pallas_call(
         functools.partial(kernel, scale),
-        out_shape=(
-            jax.ShapeDtypeStruct((4, 2, 8, 8, 8, C), BF),
-            jax.ShapeDtypeStruct((4, 2, 8, 8, 8, C), BF),
-            jax.ShapeDtypeStruct((2, 4, 28, 16, C), BF),
-            jax.ShapeDtypeStruct((2, 4, 28, 16, C), BF),
-        ),
+        out_shape=tuple(parts),
         in_specs=[
             anywhere, anywhere, pl.BlockSpec(memory_space=pltpu.SMEM), anywhere, anywhere, anywhere,
         ],
-        out_specs=(anywhere,) * 4,
+        out_specs=(anywhere,) * 5,
         scratch_shapes=[
             pltpu.VMEM(cube, BF),
             pltpu.VMEM((bricks, voxels), jnp.int32),
@@ -488,11 +579,12 @@
             pltpu.VMEM((2, 12, C, 2 * C), BF),
             face_buffer, face_buffer, face_buffer, face_buffer,
             pltpu.SemaphoreType.DMA((5,)),
-            pltpu.SemaphoreType.DMA((4,)),
+            pltpu.SemaphoreType.DMA((5,)),
             pltpu.SemaphoreType.DMA((4, 2)),
             pltpu.SemaphoreType.DMA((4, 2)),
-            *reduction,
-            *reduction,
+            *Reduction.scratch(27),
+            *Reduction.scratch(12),
+            *Reduction.scratch(15),
         ],
         compiler_params=pltpu.CompilerParams(
             collective_id=0, has_side_effects=True, vmem_limit_bytes=60 * 2**20
@@ -500,15 +592,28 @@
         name="bricks",
     )(feats.reshape(cube), mask, neighbours, weight_one, weight_two, cotangent.reshape(cube))
 
-    def unfold(g):
-        g = g[:, :, :27].transpose(2, 1, 0, 3, 4)
-        return g.reshape(27, C, C).astype(F32)
-
+    out, gin, gw1, gw2 = pl.pallas_call(
+        finish,
+        out_shape=(
+            *parts[:2],
+            jax.ShapeDtypeStruct((27, C, C), F32),
+            jax.ShapeDtypeStruct((27, C, C), F32),
+        ),
+        in_specs=[anywhere] * 5,
+        out_specs=(anywhere,) * 4,
+        scratch_shapes=[
+            *(pltpu.VMEM(p.shape, BF) for p in parts[2:]),
+            pltpu.VMEM((27, C, C), F32),
+            pltpu.VMEM((27, C, C), F32),
+            pltpu.SemaphoreType.DMA((7,)),
+        ],
+        name="outputs",
+    )(*left_over)
     return (
         out.reshape(bricks, voxels, channels),
         gin.reshape(bricks, voxels, channels),
-        unfold(gw1),
-        unfold(gw2),
+        gw1,
+        gw2,
     )
 
 

time: 105 us -> 160 us (1.52)
  Pallas kernels: 96.5 us -> 159 us
  local copies, waits for them, and re-layouts: 5.53 us -> 0 us
  other arithmetic: 1.75 us -> 0 us
    pallas_call x1 -> x2, Pallas kernels: 96.5 us -> 159 us  [the longest x1 94.6 us: body(): pl.pallas_call(functools.partial(kernel, scale), out_shape=tuple(parts),...]
    convert_element_type x2 -> x0, local copies, waits for them, and re-layouts: 2.95 us -> none  [unfold(): return g.reshape(27, C, C).astype(F32)]
    unnamed x6 -> x0, local copies, waits for them, and re-layouts: 2.57 us -> none
    convert_element_type x1 -> x0, other arithmetic: 1.75 us -> none  [unfold(): return g.reshape(27, C, C).astype(F32)]
where the time goes in v2:
time: 160 us
  Pallas kernels  159 us (99%)
    pallas_call x1, Pallas kernels, body(): pl.pallas_call(functools.partial(kernel, scale), out_shape=tuple(parts),...  94.6 us
    pallas_call x1, Pallas kernels, body(): pl.pallas_call(finish, out_shape=(*parts[:2], jax.ShapeDtypeStruct((27, C...  64.7 us

profile of v2, /device:TPU:1, one launch (start us, length us, event | category | flops | bytes accessed | tf_op | source)
XLA Modules:
  0.0 160.1 jit_solution(12706636253453355874)
XLA Ops:
  0.6 94.6 %bricks.1 = (bf16[4,2,8,8,8,128]{5,4,3,2,1,0:T(8,128)(2,1)}, bf16[4,2,8,8,8,128]{5,4,3,2,1,0:T(8,128)(2,1)}, bf16[2,16,14,8,128]{4,3,2,1,0:T(8,128)(2,1)}, bf16[...) custom-call(bf16[8,8,8,8,128]{4,3,2,1,0:T(8,128)(2,1)} %bitcast.4, s32[8,512]{1,0:T(8,128)} %mask_h.1, ...), custom_call_target="tpu_custom_call" | custom-call | tf_op jit(solution)/shard_map/bricks/pallas_call | solution.py:561
  95.3 64.7 %outputs.1 = (bf16[4,2,8,8,8,128]{5,4,3,2,1,0:T(8,128)(2,1)}, bf16[4,2,8,8,8,128]{5,4,3,2,1,0:T(8,128)(2,1)}, f32[27,128,128]{2,1,0:T(8,128)}, f32[27,128,128]{2,1,0:T(8,128)}) custom-call(bf16[4,2,8,8,8,128]{5,4,3,2,1,0:T(8,128)(2,1)} %get-tuple-element.13.out_t, bf16[4,2,8,8,8,128]{5,4,3,2,1,0:T(8,128)(2,1)} %get-tuple-element.14.gin_t, ...), custom_call_target="tpu_custom_call" | custom-call | tf_op jit(solution)/shard_map/outputs/pallas_call | solution.py:595

commit v3 on v2

--- a/solution.py
+++ b/solution.py
@@ -13,8 +13,6 @@
 C = 128
 MESH = pl.DeviceIdType.MESH
 
-A0, A7, B0, B7 = 0, 1, 2, 3
-
 
 def shifted(v):
     row = lax.broadcasted_iota(jnp.int32, v.shape, v.ndim - 1 - 1)
@@ -39,23 +37,26 @@
         ref[:, half, a] = w[:, :, half].astype(BF)
 
 
-def take_faces(x_ref, h_ref):
-    def body(p, _):
-        for half in range(2):
-            for face, cells in (
-                (A0, x_ref[p, 1, 1:9, :, C : 2 * C]),
-                (A7, x_ref[p, 8, 1:9, :, C : 2 * C]),
-                (B0, x_ref[p, 1:9, 1, :, C : 2 * C]),
-                (B7, x_ref[p, 1:9, 8, :, C : 2 * C]),
-            ):
-                v = cells.astype(F32).reshape(8, 2, 8, C)
-                h_ref[8 + 2 * p + half, face] = v[:, half].astype(BF)
-        return 0
-
-    lax.fori_loop(0, 4, body, 0)
-
-
-def fill_rim(x_ref, h_ref, nbr_ref, first):
+def keep_faces(outer, inner, a, v):
+    w = v.reshape(4, 8, 2, 8, C)
+
+    @pl.when((a == 0) | (a == 7))
+    def _():
+        for p in range(4):
+            for half in range(2):
+                outer[a // 7, 8 + 2 * p + half] = w[p, :, half].astype(BF)
+
+    @pl.when((a > 0) & (a < 7))
+    def _():
+        for p in range(4):
+            for half in range(2):
+                inner[a - 1, 8 + 2 * p + half, 0] = w[p, 0, half].astype(BF)
+                inner[a - 1, 8 + 2 * p + half, 1] = w[p, 7, half].astype(BF)
+
+
+def fill_rim(x_ref, faces, nbr_ref, first):
+    outer, inner = faces
+
     def body(p, _):
         def source(column):
             out = []
@@ -64,34 +65,28 @@
                 out.append(jnp.where(n >= 0, jnp.clip(n - first, 0, 23), 24))
             return out
 
-        def line(column, face):
-            i, j = source(column)
-            u = h_ref[i, face].astype(F32)
-            v = h_ref[j, face].astype(F32)
+        def cell(x, y, i, j):
+            w = jnp.stack([x.astype(F32), y.astype(F32)], axis=0)
+            for k, s in enumerate(shifted(w)):
+                x_ref[p, i, j, :, C * k : C * k + C] = s.reshape(16, C).astype(BF)
+
+        for column, side, where, i, j in (
+            (0, 1, 7, 0, 0), (2, 1, 0, 0, 9), (5, 0, 7, 9, 0), (7, 0, 0, 9, 9),
+        ):
+            m, n = source(column)
+            cell(outer[side, m, where], outer[side, n, where], i, j)
+        for column, side, i in ((1, 1, 0), (6, 0, 9)):
+            m, n = source(column)
+            u, v = outer[side, m].astype(F32), outer[side, n].astype(F32)
             w = jnp.stack([u, v], axis=1).reshape(16, 8, C)
-            return [s.reshape(8, 16, C).astype(BF) for s in shifted(w)]
-
-        def cell(column, face, where):
-            i, j = source(column)
-            u = h_ref[i, face, where].astype(F32)
-            v = h_ref[j, face, where].astype(F32)
-            w = jnp.stack([u, v], axis=0)
-            return [s.reshape(16, C).astype(BF) for s in shifted(w)]
-
-        for column, face, where, i, j in (
-            (0, A7, 7, 0, 0),
-            (2, A7, 0, 0, 9),
-            (5, A0, 7, 9, 0),
-            (7, A0, 0, 9, 9),
-        ):
-            for k, s in enumerate(cell(column, face, where)):
-                x_ref[p, i, j, :, C * k : C * k + C] = s
-        for column, face, i in ((1, A7, 0), (6, A0, 9)):
-            for k, s in enumerate(line(column, face)):
-                x_ref[p, i, 1:9, :, C * k : C * k + C] = s
-        for column, face, j in ((3, B7, 0), (4, B0, 9)):
-            for k, s in enumerate(line(column, face)):
-                x_ref[p, 1:9, j, :, C * k : C * k + C] = s
+            for k, s in enumerate(shifted(w)):
+                x_ref[p, i, 1:9, :, C * k : C * k + C] = s.reshape(8, 16, C).astype(BF)
+        for column, end, j in ((3, 1, 0), (4, 0, 9)):
+            m, n = source(column)
+            cell(outer[0, m, 7 * end], outer[0, n, 7 * end], 1, j)
+            for a in range(1, 7):
+                cell(inner[a - 1, m, end], inner[a - 1, n, end], 1 + a, j)
+            cell(outer[1, m, 7 * end], outer[1, n, 7 * end], 8, j)
         return 0
 
     lax.fori_loop(0, 4, body, 0)
@@ -115,7 +110,8 @@
 
 
 def convolve(x_ref, t_ref, epilogue, between=None):
-    def body(q, _):
+    def body(t, _):
+        q = jnp.where(t == 0, 0, jnp.where(t == 1, 3, t - 1))
         windows = [
             x_ref[:, 2 * q + p, k : k + 8].reshape(512, 3 * C) for p in range(4) for k in range(3)
         ]
@@ -127,7 +123,7 @@
         for u in range(2):
             epilogue(2 * q + u, total[:, C * u : C * u + C].reshape(4, 8, 16, C))
         if between is not None:
-            between(q)
+            between(t)
         return 0
 
     lax.fori_loop(0, 4, body, 0)
@@ -302,7 +298,7 @@
     out_h, gin_h, gw2_h, gw1a_h, gw1b_h,
     feats, mask, w1, w2, cot, out_s,
     xin, xhid, xg, taps, maskb, pre1, gt,
-    h0, h1, h2, h3,
+    o0, o1, o2, o3, i0, i1, i2, i3,
     load_sem, store_sem, face_send, face_recv,
     *red_refs,
 ):
@@ -347,34 +343,55 @@
     lax.fori_loop(1, 16, greet, 0)
     pl.semaphore_wait(barrier, 17)
 
-    faces = (h0, h1, h2, h3)
-
-    def face_copies(n):
-        h = faces[n]
+    faces = ((o0, i0), (o1, i1), (o2, i2), (o3, i3))
+
+    def plane_copies(n, ref, slab, a):
         return [
             pltpu.make_async_remote_copy(
-                src_ref=h.at[pl.ds(8, 8)],
-                dst_ref=h.at[pl.ds(at, 8)],
-                send_sem=face_send.at[n, side],
-                recv_sem=face_recv.at[n, side],
+                src_ref=ref.at[slab, pl.ds(8, 8)],
+                dst_ref=ref.at[slab, pl.ds(at, 8)],
+                send_sem=face_send.at[n, side, a],
+                recv_sem=face_recv.at[n, side, a],
                 device_id={"space": peer},
                 device_id_type=MESH,
             )
             for side, (at, peer) in enumerate(((0, right), (16, left)))
         ]
 
-    def send_faces(n, x_ref):
-        take_faces(x_ref, faces[n])
-        for c in face_copies(n):
-            c.start()
+    def send_plane(n, a, v):
+        outer, inner = faces[n]
+        keep_faces(outer, inner, a, v)
+
+        @pl.when((a == 0) | (a == 7))
+        def _():
+            for c in plane_copies(n, outer, a // 7, a):
+                c.start()
+
+        @pl.when((a > 0) & (a < 7))
+        def _():
+            for c in plane_copies(n, inner, a - 1, a):
+                c.start()
+
+    def face_copies(n):
+        outer, inner = faces[n]
+        copies = []
+        for a in range(8):
+            if a in (0, 7):
+                copies += plane_copies(n, outer, a // 7, a)
+            else:
+                copies += plane_copies(n, inner, a - 1, a)
+        return copies
 
     def receive_faces(n, x_ref):
         for c in face_copies(n):
             c.wait_recv()
         fill_rim(x_ref, faces[n], nbr_ref, first)
 
-    for h in faces:
-        h[24] = jnp.zeros((4, 8, 8, C), BF)
+    for outer, inner in faces:
+        for side in range(2):
+            outer[side, 24] = jnp.zeros((8, 8, C), BF)
+        for a in range(6):
+            inner[a, 24] = jnp.zeros((2, 8, C), BF)
     for red in (red2, red1a, red1b):
         red.clear()
     for side in range(2):
@@ -384,7 +401,8 @@
     loads[1].wait()
     loads[0].wait()
 
-    def mask_plane(a, _):
+    def mask_plane(t, _):
+        a = jnp.where(t == 0, 0, jnp.where(t == 1, 7, t - 1))
         row = lax.broadcasted_iota(jnp.int32, (C, C), 0)
         lane = lax.broadcasted_iota(jnp.int32, (C, C), 1)
         hit = lane == lax.rem(a, 2) * 64 + (row // 16) * 8 + lax.rem(row, 8)
@@ -400,11 +418,12 @@
         )
         m = spread.reshape(4, 8, 16, C)
         maskb[a] = m.astype(BF)
-        put_plane(xin, a, pair_plane(feats, a) * m)
+        v = pair_plane(feats, a) * m
+        send_plane(0, a, v)
+        put_plane(xin, a, v)
         return 0
 
     lax.fori_loop(0, 8, mask_plane, 0)
-    send_faces(0, xin)
 
     loads[2].wait()
     loads[3].wait()
@@ -415,10 +434,11 @@
     def first_done(a, v):
         pre1[a] = v
         s, _ = silu_parts(v)
-        put_plane(xhid, a, maskb[a].astype(F32) * (v * s))
+        h = maskb[a].astype(F32) * (v * s)
+        send_plane(1, a, h)
+        put_plane(xhid, a, h)
 
     convolve(xin, taps.at[0], first_done)
-    send_faces(1, xhid)
     build_taps(taps.at[1], w2, False)
     build_taps(taps.at[3], w1, True)
     loads[4].wait()
@@ -429,11 +449,11 @@
         m = maskb[a].astype(F32)
         unpair_plane(out_s, a, m * (v * s))
         g = pair_plane(cot, a) * m * slope
+        send_plane(2, a, g)
         put_plane(xg, a, g)
         put_transposed(gt, a, g)
 
     convolve(xhid, taps.at[1], second_done)
-    send_faces(2, xg)
     store_out = pltpu.make_async_copy(out_s, out_h, store_sem.at[0])
     store_out.start()
 
@@ -448,17 +468,16 @@
     def third_done(a, v):
         _, slope = silu_parts(pre1[a])
         g = maskb[a].astype(F32) * slope * v
+        send_plane(3, a, g)
         put_plane(xhid, a, g)
         put_transposed(gt, a, g)
 
     def third_between(q):
-        @pl.when(q == 0)
+        @pl.when(q == 1)
         def _():
             red2.step(1)
 
     convolve(xg, taps.at[2], third_done, third_between)
-    send_faces(3, xhid)
-    red2.step(2)
     store_out.wait()
 
     weight_grad(xin, gt, LEFT_COLUMNS, scale, lambda q, c, v: red1a.put(4 * (2 - q) + c, v))
@@ -466,7 +485,7 @@
     weight_grad(xin, gt, RIGHT_COLUMNS, scale, lambda q, c, v: red1b.put(5 * (2 - q) + c - 4, v))
     red1b.step(0)
     red1a.step(1)
-    red2.step(3)
+    red2.step(2)
     receive_faces(3, xhid)
     red1b.step(1)
 
@@ -474,18 +493,13 @@
         unpair_plane(out_s, a, maskb[a].astype(F32) * v)
 
     def last_between(q):
-        @pl.when(q == 1)
+        @pl.when(q == 2)
         def _():
             red1a.step(2)
 
-        @pl.when(q == 2)
+        @pl.when(q == 3)
         def _():
             red1b.step(2)
-
-        @pl.when(q == 3)
-        def _():
-            red2.step(4)
-            red1a.step(3)
 
     convolve(xhid, taps.at[3], last_done, last_between)
     stores = [
@@ -495,6 +509,9 @@
         )
     ]
     stores[0].start()
+    red2.step(3)
+    red1a.step(3)
+    red2.step(4)
     stores[1].start()
     red1b.step(3)
     red1a.step(4)
@@ -513,16 +530,13 @@
 def finish(
     out_t, gin_t, gw2_t, gw1a_t, gw1b_t,
     out_h, gin_h, gw1_h, gw2_h,
-    fin2, fin1a, fin1b, w1, w2, sem,
+    fin2, fin1a, fin1b, w1, w2, out_s, gin_s, sem,
 ):
-    copies = [
-        pltpu.make_async_copy(src, dst, sem.at[i])
-        for i, (src, dst) in enumerate(
-            ((gw2_t, fin2), (gw1a_t, fin1a), (gw1b_t, fin1b), (out_t, out_h), (gin_t, gin_h),
-             (w2, gw2_h), (w1, gw1_h))
-        )
-    ]
-    for c in copies[:5]:
+    pairs = ((gw2_t, fin2), (gw1a_t, fin1a), (gw1b_t, fin1b), (out_t, out_s), (gin_t, gin_s))
+    reads = [pltpu.make_async_copy(src, dst, sem.at[i]) for i, (src, dst) in enumerate(pairs)]
+    pairs = ((w2, gw2_h), (w1, gw1_h), (out_s, out_h), (gin_s, gin_h))
+    writes = [pltpu.make_async_copy(src, dst, sem.at[5 + i]) for i, (src, dst) in enumerate(pairs)]
+    for c in reads:
         c.start()
 
     def order(fin, tap, dst, to):
@@ -530,19 +544,22 @@
             n = 8 * tap + u // 2
             dst[to, 8 * u : 8 * u + 8] = fin[u % 2, n % 16, n // 16].astype(F32)
 
-    copies[0].wait()
+    reads[0].wait()
     for tap in range(27):
         order(fin2, tap, w2, tap)
-    copies[5].start()
-    copies[1].wait()
-    copies[2].wait()
+    writes[0].start()
+    reads[1].wait()
+    reads[2].wait()
     for k in range(3):
         for c in LEFT_COLUMNS:
             order(fin1a, 4 * k + c, w1, 9 * k + c)
         for c in RIGHT_COLUMNS:
             order(fin1b, 5 * k + c - 4, w1, 9 * k + c)
-    copies[6].start()
-    for c in copies[3:]:
+    writes[1].start()
+    for i in (3, 4):
+        reads[i].wait()
+        writes[i - 1].start()
+    for c in writes:
         c.wait()
 
 
@@ -551,7 +568,7 @@
     scale = 1.0 / math.sqrt(voxels * bricks)
     cube = (bricks, 8, 8, 8, channels)
     field = pltpu.VMEM((4, 10, 10, 16, 3 * C), BF)
-    face_buffer = pltpu.VMEM((25, 4, 8, 8, C), BF)
+    outer, inner = pltpu.VMEM((2, 25, 8, 8, C), BF), pltpu.VMEM((6, 25, 2, 8, C), BF)
     anywhere = pl.BlockSpec(memory_space=pl.ANY)
     parts = [
         jax.ShapeDtypeStruct((4, 2, 8, 8, 8, C), BF),
@@ -577,11 +594,12 @@
             pltpu.VMEM((8, 4, 8, 16, C), BF),
             pltpu.VMEM((8, 4, 8, 16, C), F32),
             pltpu.VMEM((2, 12, C, 2 * C), BF),
-            face_buffer, face_buffer, face_buffer, face_buffer,
+            *[outer] * 4,
+            *[inner] * 4,
             pltpu.SemaphoreType.DMA((5,)),
             pltpu.SemaphoreType.DMA((5,)),
-            pltpu.SemaphoreType.DMA((4, 2)),
-            pltpu.SemaphoreType.DMA((4, 2)),
+            pltpu.SemaphoreType.DMA((4, 2, 8)),
+            pltpu.SemaphoreType.DMA((4, 2, 8)),
             *Reduction.scratch(27),
             *Reduction.scratch(12),
             *Reduction.scratch(15),
@@ -605,7 +623,9 @@
             *(pltpu.VMEM(p.shape, BF) for p in parts[2:]),
             pltpu.VMEM((27, C, C), F32),
             pltpu.VMEM((27, C, C), F32),
-            pltpu.SemaphoreType.DMA((7,)),
+            pltpu.VMEM(parts[0].shape, BF),
+            pltpu.VMEM(parts[1].shape, BF),
+            pltpu.SemaphoreType.DMA((9,)),
         ],
         name="outputs",
     )(*left_over)

time: 160 us -> 85.3 us (0.53)
  Pallas kernels: 159 us -> 84.3 us
    pallas_call x1, Pallas kernels: 64.7 us -> 3.85 us  [body(): pl.pallas_call(finish, out_shape=(*parts[:2], jax.ShapeDtypeStruct((27, C...]
    pallas_call x1, Pallas kernels: 94.6 us -> 80.5 us  [body(): pl.pallas_call(functools.partial(kernel, scale), out_shape=tuple(parts),...]
where the time goes in v3:
time: 85.3 us; the launch traced here: 85.1 us
  Pallas kernels  84.3 us (99%)
    pallas_call x1, Pallas kernels, body(): pl.pallas_call(functools.partial(kernel, scale), out_shape=tuple(parts),...  80.5 us
    pallas_call x1, Pallas kernels, body(): pl.pallas_call(finish, out_shape=(*parts[:2], jax.ShapeDtypeStruct((27, C...  3.85 us

profile of v3, /device:TPU:1, one launch (start us, length us, event | category | flops | bytes accessed | tf_op | source)
XLA Modules:
  0.0 85.1 jit_solution(3484081326619310004)
XLA Ops:
  0.6 80.5 %bricks.1 = (bf16[4,2,8,8,8,128]{5,4,3,2,1,0:T(8,128)(2,1)}, bf16[4,2,8,8,8,128]{5,4,3,2,1,0:T(8,128)(2,1)}, bf16[2,16,14,8,128]{4,3,2,1,0:T(8,128)(2,1)}, bf16[...) custom-call(bf16[8,8,8,8,128]{4,3,2,1,0:T(8,128)(2,1)} %bitcast.4, s32[8,512]{1,0:T(8,128)} %mask_h.1, ...), custom_call_target="tpu_custom_call" | custom-call | tf_op jit(solution)/shard_map/bricks/pallas_call | solution.py:578
  81.1 3.9 %outputs.1 = (bf16[4,2,8,8,8,128]{5,4,3,2,1,0:T(8,128)(2,1)}, bf16[4,2,8,8,8,128]{5,4,3,2,1,0:T(8,128)(2,1)}, f32[27,128,128]{2,1,0:T(8,128)}, f32[27,128,128]{2,1,0:T(8,128)}) custom-call(bf16[4,2,8,8,8,128]{5,4,3,2,1,0:T(8,128)(2,1)} %get-tuple-element.13.out_t, bf16[4,2,8,8,8,128]{5,4,3,2,1,0:T(8,128)(2,1)} %get-tuple-element.14.gin_t, ...), custom_call_target="tpu_custom_call" | custom-call | tf_op jit(solution)/shard_map/outputs/pallas_call | solution.py:613

commit v4 on v3

--- a/solution.py
+++ b/solution.py
@@ -37,21 +37,29 @@
         ref[:, half, a] = w[:, :, half].astype(BF)
 
 
+def when_outer(a, run_outer, run_inner):
+    if isinstance(a, int):
+        run_outer() if a in (0, 7) else run_inner()
+        return
+    pl.when((a == 0) | (a == 7))(run_outer)
+    pl.when((a > 0) & (a < 7))(run_inner)
+
+
 def keep_faces(outer, inner, a, v):
     w = v.reshape(4, 8, 2, 8, C)
 
-    @pl.when((a == 0) | (a == 7))
-    def _():
+    def whole():
         for p in range(4):
             for half in range(2):
                 outer[a // 7, 8 + 2 * p + half] = w[p, :, half].astype(BF)
 
-    @pl.when((a > 0) & (a < 7))
-    def _():
+    def ends():
         for p in range(4):
             for half in range(2):
                 inner[a - 1, 8 + 2 * p + half, 0] = w[p, 0, half].astype(BF)
                 inner[a - 1, 8 + 2 * p + half, 1] = w[p, 7, half].astype(BF)
+
+    when_outer(a, whole, ends)
 
 
 def fill_rim(x_ref, faces, nbr_ref, first):
@@ -129,6 +137,43 @@
     lax.fori_loop(0, 4, body, 0)
 
 
+def convolve_split(x_ref, t_ref, inner_ref, arrive, epilogue):
+    def pair(q):
+        windows = [
+            x_ref[:, 2 * q + p, k : k + 8].reshape(512, 3 * C) for p in range(4) for k in range(3)
+        ]
+        total = jnp.dot(
+            jnp.concatenate(windows, axis=1),
+            t_ref[...].reshape(36 * C, 2 * C),
+            preferred_element_type=F32,
+        )
+        return [total[:, C * u : C * u + C].reshape(4, 8, 16, C) for u in range(2)]
+
+    def early(t, _):
+        for u, v in enumerate(pair(1 + t)):
+            inner_ref[2 * t + u] = v
+        return 0
+
+    lax.fori_loop(0, 2, early, 0)
+    arrive()
+    for end, column, k in ((0, 0, 0), (7, 9, 2)):
+        left = [x_ref[:, 2 + p : 6 + p, column].reshape(256, 3 * C) for p in range(3)]
+        right = [t_ref[9 * p + 3 * k : 9 * p + 3 * k + 3, :, :C].reshape(3 * C, C) for p in range(3)]
+        d = jnp.dot(
+            jnp.concatenate(left, axis=1),
+            jnp.concatenate(right, axis=0),
+            preferred_element_type=F32,
+        ).reshape(4, 4, 16, C)
+        for a in range(4):
+            inner_ref[a, :, end] += d[:, a]
+    for t in range(2):
+        outer = pair(3 * t)
+        for u in range(2):
+            epilogue(2 + 2 * t + u, inner_ref[2 * t + u])
+        for u in range(2):
+            epilogue(6 * t + u, outer[u])
+
+
 def put_transposed(gt_ref, a, v):
     flat = v.reshape(4, C, C)
     for p in range(4):
@@ -295,13 +340,14 @@
 def kernel(
     scale,
     feats_h, mask_h, nbr_ref, w1_h, w2_h, cot_h,
-    out_h, gin_h, gw2_h, gw1a_h, gw1b_h,
+    out_h, gin_h, gw2a_h, gw2b_h, gw1a_h, gw1b_h,
     feats, mask, w1, w2, cot, out_s,
-    xin, xhid, xg, taps, maskb, pre1, gt,
+    xin, xhid, xg, taps, maskb, pre1, early, gt,
     o0, o1, o2, o3, i0, i1, i2, i3,
     load_sem, store_sem, face_send, face_recv,
     *red_refs,
 ):
+    grads_h = (gw2a_h, gw2b_h, gw1a_h, gw1b_h)
     me = lax.axis_index("space")
     n_space = 32
     core = lax.rem(me, 2)
@@ -318,9 +364,10 @@
 
     place = {"core": core, "sibling": me + 1 - 2 * core, "chip": chip_at, "behind": behind}
     first = 8 * (me - 1)
-    red2 = Reduction(place, 27, red_refs[:7])
-    red1a = Reduction(place, 12, red_refs[7:14])
-    red1b = Reduction(place, 15, red_refs[14:])
+    red2a, red2b, red1a, red1b = (
+        Reduction(place, taps_of, red_refs[7 * i : 7 * i + 7])
+        for i, taps_of in enumerate((12, 15, 12, 15))
+    )
 
     loads = [
         pltpu.make_async_copy(src, dst, load_sem.at[i])
@@ -362,15 +409,11 @@
         outer, inner = faces[n]
         keep_faces(outer, inner, a, v)
 
-        @pl.when((a == 0) | (a == 7))
-        def _():
-            for c in plane_copies(n, outer, a // 7, a):
+        def start(ref, slab):
+            for c in plane_copies(n, ref, slab, a):
                 c.start()
 
-        @pl.when((a > 0) & (a < 7))
-        def _():
-            for c in plane_copies(n, inner, a - 1, a):
-                c.start()
+        when_outer(a, lambda: start(outer, a // 7), lambda: start(inner, a - 1))
 
     def face_copies(n):
         outer, inner = faces[n]
@@ -392,11 +435,15 @@
             outer[side, 24] = jnp.zeros((8, 8, C), BF)
         for a in range(6):
             inner[a, 24] = jnp.zeros((2, 8, C), BF)
-    for red in (red2, red1a, red1b):
+    for red in (red2a, red2b, red1a, red1b):
         red.clear()
     for side in range(2):
         for a in (0, 1, 10, 11):
             gt[side, a] = jnp.zeros((C, 2 * C), BF)
+
+    for x_ref in (xin, xhid):
+        for column in (0, 9):
+            x_ref[:, :, column] = jnp.zeros((4, 10, 16, 3 * C), BF)
 
     loads[1].wait()
     loads[0].wait()
@@ -429,8 +476,6 @@
     loads[3].wait()
     build_taps(taps.at[0], w1, False)
     build_taps(taps.at[2], w2, True)
-    receive_faces(0, xin)
-
     def first_done(a, v):
         pre1[a] = v
         s, _ = silu_parts(v)
@@ -438,11 +483,10 @@
         send_plane(1, a, h)
         put_plane(xhid, a, h)
 
-    convolve(xin, taps.at[0], first_done)
+    convolve_split(xin, taps.at[0], early, lambda: receive_faces(0, xin), first_done)
     build_taps(taps.at[1], w2, False)
     build_taps(taps.at[3], w1, True)
     loads[4].wait()
-    receive_faces(1, xhid)
 
     def second_done(a, v):
         s, slope = silu_parts(v)
@@ -453,16 +497,15 @@
         put_plane(xg, a, g)
         put_transposed(gt, a, g)
 
-    convolve(xhid, taps.at[1], second_done)
+    convolve_split(xhid, taps.at[1], early, lambda: receive_faces(1, xhid), second_done)
     store_out = pltpu.make_async_copy(out_s, out_h, store_sem.at[0])
     store_out.start()
 
-    def put_w2(q, c, block):
-        red2.put(9 * (2 - q) + c, block)
-
-    weight_grad(xhid, gt, LEFT_COLUMNS, scale, put_w2)
-    weight_grad(xhid, gt, RIGHT_COLUMNS, scale, put_w2)
-    red2.step(0)
+    weight_grad(xhid, gt, LEFT_COLUMNS, scale, lambda q, c, v: red2a.put(4 * (2 - q) + c, v))
+    red2a.step(0)
+    weight_grad(xhid, gt, RIGHT_COLUMNS, scale, lambda q, c, v: red2b.put(5 * (2 - q) + c - 4, v))
+    red2b.step(0)
+    red2a.step(1)
     receive_faces(2, xg)
 
     def third_done(a, v):
@@ -473,19 +516,23 @@
         put_transposed(gt, a, g)
 
     def third_between(q):
-        @pl.when(q == 1)
+        @pl.when(q == 0)
         def _():
-            red2.step(1)
+            red2b.step(1)
+
+        @pl.when(q == 3)
+        def _():
+            red2a.step(2)
 
     convolve(xg, taps.at[2], third_done, third_between)
     store_out.wait()
 
     weight_grad(xin, gt, LEFT_COLUMNS, scale, lambda q, c, v: red1a.put(4 * (2 - q) + c, v))
     red1a.step(0)
+    red2b.step(2)
     weight_grad(xin, gt, RIGHT_COLUMNS, scale, lambda q, c, v: red1b.put(5 * (2 - q) + c - 4, v))
     red1b.step(0)
     red1a.step(1)
-    red2.step(2)
     receive_faces(3, xhid)
     red1b.step(1)
 
@@ -493,6 +540,10 @@
         unpair_plane(out_s, a, maskb[a].astype(F32) * v)
 
     def last_between(q):
+        @pl.when(q == 1)
+        def _():
+            red2a.step(3)
+
         @pl.when(q == 2)
         def _():
             red1a.step(2)
@@ -502,40 +553,46 @@
             red1b.step(2)
 
     convolve(xhid, taps.at[3], last_done, last_between)
+    reductions = (red2a, red2b, red1a, red1b)
     stores = [
         pltpu.make_async_copy(src, dst, store_sem.at[1 + i])
         for i, (src, dst) in enumerate(
-            ((out_s, gin_h), (red2.fin, gw2_h), (red1a.fin, gw1a_h), (red1b.fin, gw1b_h))
+            ((out_s, gin_h), *((red.fin, dst) for red, dst in zip(reductions, grads_h)))
         )
     ]
     stores[0].start()
-    red2.step(3)
+    red2b.step(3)
     red1a.step(3)
-    red2.step(4)
+    red2a.step(4)
     stores[1].start()
+    red2b.step(4)
+    stores[2].start()
     red1b.step(3)
     red1a.step(4)
-    stores[2].start()
+    stores[3].start()
     red1b.step(4)
-    stores[3].start()
+    stores[4].start()
     for n in range(4):
         for c in face_copies(n):
             c.wait_send()
-    for red in (red2, red1a, red1b):
+    for red in (red2a, red2b, red1a, red1b):
         red.drain()
     for c in stores:
         c.wait()
 
 
 def finish(
-    out_t, gin_t, gw2_t, gw1a_t, gw1b_t,
+    out_t, gin_t, gw2a_t, gw2b_t, gw1a_t, gw1b_t,
     out_h, gin_h, gw1_h, gw2_h,
-    fin2, fin1a, fin1b, w1, w2, out_s, gin_s, sem,
+    fin2a, fin2b, fin1a, fin1b, w1, w2, out_s, gin_s, sem,
 ):
-    pairs = ((gw2_t, fin2), (gw1a_t, fin1a), (gw1b_t, fin1b), (out_t, out_s), (gin_t, gin_s))
+    pairs = (
+        (gw2a_t, fin2a), (gw2b_t, fin2b), (gw1a_t, fin1a), (gw1b_t, fin1b),
+        (out_t, out_s), (gin_t, gin_s),
+    )
     reads = [pltpu.make_async_copy(src, dst, sem.at[i]) for i, (src, dst) in enumerate(pairs)]
     pairs = ((w2, gw2_h), (w1, gw1_h), (out_s, out_h), (gin_s, gin_h))
-    writes = [pltpu.make_async_copy(src, dst, sem.at[5 + i]) for i, (src, dst) in enumerate(pairs)]
+    writes = [pltpu.make_async_copy(src, dst, sem.at[6 + i]) for i, (src, dst) in enumerate(pairs)]
     for c in reads:
         c.start()
 
@@ -544,21 +601,18 @@
             n = 8 * tap + u // 2
             dst[to, 8 * u : 8 * u + 8] = fin[u % 2, n % 16, n // 16].astype(F32)
 
-    reads[0].wait()
-    for tap in range(27):
-        order(fin2, tap, w2, tap)
-    writes[0].start()
-    reads[1].wait()
-    reads[2].wait()
-    for k in range(3):
-        for c in LEFT_COLUMNS:
-            order(fin1a, 4 * k + c, w1, 9 * k + c)
-        for c in RIGHT_COLUMNS:
-            order(fin1b, 5 * k + c - 4, w1, 9 * k + c)
-    writes[1].start()
-    for i in (3, 4):
+    for i, (left, right, dst) in enumerate(((fin2a, fin2b, w2), (fin1a, fin1b, w1))):
+        reads[2 * i].wait()
+        reads[2 * i + 1].wait()
+        for k in range(3):
+            for c in LEFT_COLUMNS:
+                order(left, 4 * k + c, dst, 9 * k + c)
+            for c in RIGHT_COLUMNS:
+                order(right, 5 * k + c - 4, dst, 9 * k + c)
+        writes[i].start()
+    for i in (4, 5):
         reads[i].wait()
-        writes[i - 1].start()
+        writes[i - 2].start()
     for c in writes:
         c.wait()
 
@@ -573,7 +627,7 @@
     parts = [
         jax.ShapeDtypeStruct((4, 2, 8, 8, 8, C), BF),
         jax.ShapeDtypeStruct((4, 2, 8, 8, 8, C), BF),
-        *(jax.ShapeDtypeStruct((2, 16, slots_of(n), 8, C), BF) for n in (27, 12, 15)),
+        *(jax.ShapeDtypeStruct((2, 16, slots_of(n), 8, C), BF) for n in (12, 15, 12, 15)),
     ]
     left_over = pl.pallas_call(
         functools.partial(kernel, scale),
@@ -581,7 +635,7 @@
         in_specs=[
             anywhere, anywhere, pl.BlockSpec(memory_space=pltpu.SMEM), anywhere, anywhere, anywhere,
         ],
-        out_specs=(anywhere,) * 5,
+        out_specs=(anywhere,) * 6,
         scratch_shapes=[
             pltpu.VMEM(cube, BF),
             pltpu.VMEM((bricks, voxels), jnp.int32),
@@ -593,16 +647,15 @@
             pltpu.VMEM((4, 36, C, 2 * C), BF),
             pltpu.VMEM((8, 4, 8, 16, C), BF),
             pltpu.VMEM((8, 4, 8, 16, C), F32),
+            pltpu.VMEM((4, 4, 8, 16, C), F32),
             pltpu.VMEM((2, 12, C, 2 * C), BF),
             *[outer] * 4,
             *[inner] * 4,
             pltpu.SemaphoreType.DMA((5,)),
-            pltpu.SemaphoreType.DMA((5,)),
+            pltpu.SemaphoreType.DMA((6,)),
             pltpu.SemaphoreType.DMA((4, 2, 8)),
             pltpu.SemaphoreType.DMA((4, 2, 8)),
-            *Reduction.scratch(27),
-            *Reduction.scratch(12),
-            *Reduction.scratch(15),
+            *(ref for n in (12, 15, 12, 15) for ref in Reduction.scratch(n)),
         ],
         compiler_params=pltpu.CompilerParams(
             collective_id=0, has_side_effects=True, vmem_limit_bytes=60 * 2**20
@@ -617,7 +670,7 @@
             jax.ShapeDtypeStruct((27, C, C), F32),
             jax.ShapeDtypeStruct((27, C, C), F32),
         ),
-        in_specs=[anywhere] * 5,
+        in_specs=[anywhere] * 6,
         out_specs=(anywhere,) * 4,
         scratch_shapes=[
             *(pltpu.VMEM(p.shape, BF) for p in parts[2:]),
@@ -625,7 +678,7 @@
             pltpu.VMEM((27, C, C), F32),
             pltpu.VMEM(parts[0].shape, BF),
             pltpu.VMEM(parts[1].shape, BF),
-            pltpu.SemaphoreType.DMA((9,)),
+            pltpu.SemaphoreType.DMA((10,)),
         ],
         name="outputs",
     )(*left_over)

time: 85.3 us -> 84.7 us (level)
  no operation moved by 1% of the time
where the time goes in v4:
time: 84.7 us; the launch traced here: 84.5 us
  Pallas kernels  83.7 us (99%)
    pallas_call x1, Pallas kernels, body(): pl.pallas_call(functools.partial(kernel, scale), out_shape=tuple(parts),...  79.9 us
    pallas_call x1, Pallas kernels, body(): pl.pallas_call(finish, out_shape=(*parts[:2], jax.ShapeDtypeStruct((27, C...  3.85 us

profile of v4, /device:TPU:1, one launch (start us, length us, event | category | flops | bytes accessed | tf_op | source)
XLA Modules:
  0.0 84.5 jit_solution(5721023847143680992)
XLA Ops:
  0.6 79.9 %bricks.1 = (bf16[4,2,8,8,8,128]{5,4,3,2,1,0:T(8,128)(2,1)}, bf16[4,2,8,8,8,128]{5,4,3,2,1,0:T(8,128)(2,1)}, bf16[2,16,6,8,128]{4,3,2,1,0:T(8,128)(2,1)}, bf16[2...) custom-call(bf16[8,8,8,8,128]{4,3,2,1,0:T(8,128)(2,1)} %bitcast.4, ...), custom_call_target="tpu_custom_call" | custom-call | tf_op jit(solution)/shard_map/bricks/pallas_call | solution.py:632
  80.5 3.8 %outputs.1 = (bf16[4,2,8,8,8,128]{5,4,3,2,1,0:T(8,128)(2,1)}, bf16[4,2,8,8,8,128]{5,4,3,2,1,0:T(8,128)(2,1)}, f32[27,128,128]{2,1,0:T(8,128)}, f32[27,128,128]{2,1,0:T(8,128)}) custom-call(bf16[4,2,8,8,8,128]{5,4,3,2,1,0:T(8,128)(2,1)} %get-tuple-element.14.out_t, bf16[4,2,8,8,8,128]{5,4,3,2,1,0:T(8,128)(2,1)} %get-tuple-element.15.gin_t, ...), custom_call_target="tpu_custom_call" | custom-call | tf_op jit(solution)/shard_map/outputs/pallas_call | solution.py:666

commit v5 on v4

--- a/solution.py
+++ b/solution.py
@@ -520,33 +520,35 @@
         def _():
             red2b.step(1)
 
+        @pl.when(q == 2)
+        def _():
+            red2a.step(2)
+
         @pl.when(q == 3)
         def _():
-            red2a.step(2)
+            red2b.step(2)
 
     convolve(xg, taps.at[2], third_done, third_between)
     store_out.wait()
 
+    weight_grad(xin, gt, RIGHT_COLUMNS, scale, lambda q, c, v: red1b.put(5 * (2 - q) + c - 4, v))
+    red1b.step(0)
     weight_grad(xin, gt, LEFT_COLUMNS, scale, lambda q, c, v: red1a.put(4 * (2 - q) + c, v))
     red1a.step(0)
-    red2b.step(2)
-    weight_grad(xin, gt, RIGHT_COLUMNS, scale, lambda q, c, v: red1b.put(5 * (2 - q) + c - 4, v))
-    red1b.step(0)
-    red1a.step(1)
+    red1b.step(1)
     receive_faces(3, xhid)
-    red1b.step(1)
 
     def last_done(a, v):
         unpair_plane(out_s, a, maskb[a].astype(F32) * v)
 
     def last_between(q):
-        @pl.when(q == 1)
+        @pl.when(q == 0)
+        def _():
+            red1a.step(1)
+
+        @pl.when(q == 2)
         def _():
             red2a.step(3)
-
-        @pl.when(q == 2)
-        def _():
-            red1a.step(2)
 
         @pl.when(q == 3)
         def _():
@@ -561,17 +563,18 @@
         )
     ]
     stores[0].start()
+    red1a.step(2)
     red2b.step(3)
-    red1a.step(3)
     red2a.step(4)
     stores[1].start()
     red2b.step(4)
     stores[2].start()
     red1b.step(3)
+    red1a.step(3)
+    red1b.step(4)
+    stores[4].start()
     red1a.step(4)
     stores[3].start()
-    red1b.step(4)
-    stores[4].start()
     for n in range(4):
         for c in face_copies(n):
             c.wait_send()

time: 84.7 us -> 90.2 us (1.065)
  Pallas kernels: 83.7 us -> 89.3 us
    pallas_call x1, Pallas kernels: 79.9 us -> 85.4 us  [body(): pl.pallas_call(functools.partial(kernel, scale), out_shape=tuple(parts),...]
where the time goes in v5:
time: 90.2 us; the launch traced here: 90.1 us
  Pallas kernels  89.3 us (99%)
    pallas_call x1, Pallas kernels, body(): pl.pallas_call(functools.partial(kernel, scale), out_shape=tuple(parts),...  85.4 us
    pallas_call x1, Pallas kernels, body(): pl.pallas_call(finish, out_shape=(*parts[:2], jax.ShapeDtypeStruct((27, C...  3.85 us

profile of v5, /device:TPU:1, one launch (start us, length us, event | category | flops | bytes accessed | tf_op | source)
XLA Modules:
  0.0 90.1 jit_solution(12258294090517497177)
XLA Ops:
  0.6 85.4 %bricks.1 = (bf16[4,2,8,8,8,128]{5,4,3,2,1,0:T(8,128)(2,1)}, bf16[4,2,8,8,8,128]{5,4,3,2,1,0:T(8,128)(2,1)}, bf16[2,16,6,8,128]{4,3,2,1,0:T(8,128)(2,1)}, bf16[2...) custom-call(bf16[8,8,8,8,128]{4,3,2,1,0:T(8,128)(2,1)} %bitcast.4, ...), custom_call_target="tpu_custom_call" | custom-call | tf_op jit(solution)/shard_map/bricks/pallas_call | solution.py:635
  86.1 3.8 %outputs.1 = (bf16[4,2,8,8,8,128]{5,4,3,2,1,0:T(8,128)(2,1)}, bf16[4,2,8,8,8,128]{5,4,3,2,1,0:T(8,128)(2,1)}, f32[27,128,128]{2,1,0:T(8,128)}, f32[27,128,128]{2,1,0:T(8,128)}) custom-call(bf16[4,2,8,8,8,128]{5,4,3,2,1,0:T(8,128)(2,1)} %get-tuple-element.14.out_t, bf16[4,2,8,8,8,128]{5,4,3,2,1,0:T(8,128)(2,1)} %get-tuple-element.15.gin_t, ...), custom_call_target="tpu_custom_call" | custom-call | tf_op jit(solution)/shard_map/outputs/pallas_call | solution.py:669

commit v6 on v5

--- a/solution.py
+++ b/solution.py
@@ -332,6 +332,81 @@
         lax.fori_loop(1, 16, body, 0)
 
 
+class TwoLevel(Reduction):
+    @staticmethod
+    def scratch(taps):
+        n = slots_of(taps)
+        return [
+            pltpu.VMEM((2, 16, n, 8, C), BF),
+            pltpu.VMEM((16, n, 8, C), BF),
+            pltpu.VMEM((16, n, 8, C), BF),
+            pltpu.VMEM((19, n, 8, C), BF),
+            pltpu.VMEM((2, 16, n, 8, C), BF),
+            pltpu.SemaphoreType.DMA((14,)),
+            pltpu.SemaphoreType.DMA((14,)),
+        ]
+
+    def phase(self, n):
+        p = self.place
+        core, y, z, me = p["core"], p["y"], p["z"], p["me"]
+        if n == 0:
+            return [self.pair()]
+        if n == 5:
+            return [self.copy(self.fin.at[core], self.fin.at[core], 13, p["sibling"])]
+        copies = []
+        for d in range(3):
+            yd, zd = lax.rem(y + d + 1, 4), lax.rem(z + d + 1, 4)
+            above, beside = me + (yd - y) * 8, me + (zd - z) * 2
+            if n == 1:
+                src, dst = self.s0.at[pl.ds(4 * yd, 4)], self.r1.at[pl.ds(4 * d, 4)]
+                copies.append(self.copy(src, dst, 1 + d, above))
+            elif n == 2:
+                copies.append(self.copy(self.r1.at[12 + zd], self.r1.at[16 + d], 4 + d, beside))
+            elif n == 3:
+                one = self.fin.at[core, 4 * y + z]
+                copies.append(self.copy(one, one, 7 + d, beside))
+            else:
+                row = self.fin.at[core, pl.ds(4 * y, 4)]
+                copies.append(self.copy(row, row, 10 + d, above))
+        return copies
+
+    def step(self, n):
+        p = self.place
+        core, y, z = p["core"], p["y"], p["z"]
+        if n > 0:
+            for c in self.phase(n - 1):
+                c.wait_recv()
+        if n == 1:
+
+            def add(i, _):
+                self.s0[i] = (self.g[core, i].astype(F32) + self.r0[i].astype(F32)).astype(BF)
+                return 0
+
+            lax.fori_loop(0, 16, add, 0)
+        elif n == 2:
+            for i in range(4):
+                v = self.s0[4 * y + i].astype(F32)
+                for d in range(3):
+                    v = v + self.r1[4 * d + i].astype(F32)
+                self.r1[12 + i] = v.astype(BF)
+        elif n == 3:
+            v = self.r1[12 + z].astype(F32)
+            for d in range(3):
+                v = v + self.r1[16 + d].astype(F32)
+            self.fin[core, 4 * y + z] = v.astype(BF)
+        if n < 6:
+            for c in self.phase(n):
+                c.start()
+
+    def drain(self):
+        for n in range(6):
+            for c in self.phase(n):
+                c.wait_send()
+
+
+REDUCTIONS = ((TwoLevel, 12), (TwoLevel, 15), (Reduction, 12), (Reduction, 15))
+
+
 def silu_parts(v):
     s = 1.0 / (1.0 + jnp.exp(-v))
     return s, s * (1.0 + v * (1.0 - s))
@@ -362,11 +437,14 @@
     def behind(d):
         return 4 * lax.rem(y + 4 - d // 4, 4) + lax.rem(z + 4 - lax.rem(d, 4), 4)
 
-    place = {"core": core, "sibling": me + 1 - 2 * core, "chip": chip_at, "behind": behind}
+    place = {
+        "core": core, "sibling": me + 1 - 2 * core, "chip": chip_at, "behind": behind,
+        "y": y, "z": z, "me": me,
+    }
     first = 8 * (me - 1)
     red2a, red2b, red1a, red1b = (
-        Reduction(place, taps_of, red_refs[7 * i : 7 * i + 7])
-        for i, taps_of in enumerate((12, 15, 12, 15))
+        kind(place, taps_of, red_refs[7 * i : 7 * i + 7])
+        for i, (kind, taps_of) in enumerate(REDUCTIONS)
     )
 
     loads = [
@@ -516,7 +594,7 @@
         put_transposed(gt, a, g)
 
     def third_between(q):
-        @pl.when(q == 0)
+        @pl.when(q == 1)
         def _():
             red2b.step(1)
 
@@ -524,19 +602,18 @@
         def _():
             red2a.step(2)
 
-        @pl.when(q == 3)
-        def _():
-            red2b.step(2)
-
     convolve(xg, taps.at[2], third_done, third_between)
     store_out.wait()
 
     weight_grad(xin, gt, RIGHT_COLUMNS, scale, lambda q, c, v: red1b.put(5 * (2 - q) + c - 4, v))
     red1b.step(0)
+    red2a.step(3)
+    red2b.step(2)
     weight_grad(xin, gt, LEFT_COLUMNS, scale, lambda q, c, v: red1a.put(4 * (2 - q) + c, v))
     red1a.step(0)
     red1b.step(1)
     receive_faces(3, xhid)
+    red2a.step(4)
 
     def last_done(a, v):
         unpair_plane(out_s, a, maskb[a].astype(F32) * v)
@@ -545,13 +622,11 @@
         @pl.when(q == 0)
         def _():
             red1a.step(1)
-
-        @pl.when(q == 2)
-        def _():
-            red2a.step(3)
+            red2b.step(3)
 
         @pl.when(q == 3)
         def _():
+            red2b.step(4)
             red1b.step(2)
 
     convolve(xhid, taps.at[3], last_done, last_between)
@@ -564,12 +639,13 @@
     ]
     stores[0].start()
     red1a.step(2)
-    red2b.step(3)
-    red2a.step(4)
+    red2a.step(5)
+    red2a.step(6)
     stores[1].start()
-    red2b.step(4)
+    red2b.step(5)
+    red1b.step(3)
+    red2b.step(6)
     stores[2].start()
-    red1b.step(3)
     red1a.step(3)
     red1b.step(4)
     stores[4].start()
@@ -630,7 +706,7 @@
     parts = [
         jax.ShapeDtypeStruct((4, 2, 8, 8, 8, C), BF),
         jax.ShapeDtypeStruct((4, 2, 8, 8, 8, C), BF),
-        *(jax.ShapeDtypeStruct((2, 16, slots_of(n), 8, C), BF) for n in (12, 15, 12, 15)),
+        *(jax.ShapeDtypeStruct((2, 16, slots_of(n), 8, C), BF) for _, n in REDUCTIONS),
     ]
     left_over = pl.pallas_call(
         functools.partial(kernel, scale),
@@ -658,7 +734,7 @@
             pltpu.SemaphoreType.DMA((6,)),
             pltpu.SemaphoreType.DMA((4, 2, 8)),
             pltpu.SemaphoreType.DMA((4, 2, 8)),
-            *(ref for n in (12, 15, 12, 15) for ref in Reduction.scratch(n)),
+            *(ref for kind, n in REDUCTIONS for ref in kind.scratch(n)),
         ],
         compiler_params=pltpu.CompilerParams(
             collective_id=0, has_side_effects=True, vmem_limit_bytes=60 * 2**20

time: 90.2 us -> 87.1 us (0.966)
  Pallas kernels: 89.3 us -> 86.2 us
    pallas_call x1, Pallas kernels: 85.4 us -> 82.3 us  [body(): pl.pallas_call(functools.partial(kernel, scale), out_shape=tuple(parts),...]
where the time goes in v6:
time: 87.1 us; the launch traced here: 87 us
  Pallas kernels  86.2 us (99%)
    pallas_call x1, Pallas kernels, body(): pl.pallas_call(functools.partial(kernel, scale), out_shape=tuple(parts),...  82.3 us
    pallas_call x1, Pallas kernels, body(): pl.pallas_call(finish, out_shape=(*parts[:2], jax.ShapeDtypeStruct((27, C...  3.85 us

profile of v6, /device:TPU:1, one launch (start us, length us, event | category | flops | bytes accessed | tf_op | source)
XLA Modules:
  0.0 87.0 jit_solution(7900847981680621309)
XLA Ops:
  0.6 82.3 %bricks.1 = (bf16[4,2,8,8,8,128]{5,4,3,2,1,0:T(8,128)(2,1)}, bf16[4,2,8,8,8,128]{5,4,3,2,1,0:T(8,128)(2,1)}, bf16[2,16,6,8,128]{4,3,2,1,0:T(8,128)(2,1)}, bf16[2...) custom-call(bf16[8,8,8,8,128]{4,3,2,1,0:T(8,128)(2,1)} %bitcast.4, ...), custom_call_target="tpu_custom_call" | custom-call | tf_op jit(solution)/shard_map/bricks/pallas_call | solution.py:711
  83.0 3.8 %outputs.1 = (bf16[4,2,8,8,8,128]{5,4,3,2,1,0:T(8,128)(2,1)}, bf16[4,2,8,8,8,128]{5,4,3,2,1,0:T(8,128)(2,1)}, f32[27,128,128]{2,1,0:T(8,128)}, f32[27,128,128]{2,1,0:T(8,128)}) custom-call(bf16[4,2,8,8,8,128]{5,4,3,2,1,0:T(8,128)(2,1)} %get-tuple-element.14.out_t, bf16[4,2,8,8,8,128]{5,4,3,2,1,0:T(8,128)(2,1)} %get-tuple-element.15.gin_t, ...), custom_call_target="tpu_custom_call" | custom-call | tf_op jit(solution)/shard_map/outputs/pallas_call | solution.py:745

commit v7 on v4

--- a/solution.py
+++ b/solution.py
@@ -107,7 +107,7 @@
         t_ref[27 + t, :, :C] = zero
         for k in range(3):
             if flipped:
-                w = w_ref[26 - (9 * k + t)].astype(F32).T.astype(BF)
+                w = w_ref[26 - (9 * k + t)].T
             else:
                 w = w_ref[9 * k + t]
             t_ref[9 * k + t, :, :C] = w
@@ -175,9 +175,9 @@
 
 
 def put_transposed(gt_ref, a, v):
-    flat = v.reshape(4, C, C)
+    flat = v.reshape(4, C, C).astype(BF)
     for p in range(4):
-        gt_ref[p // 2, a + 2, :, C * (p % 2) : C * (p % 2) + C] = flat[p].T.astype(BF)
+        gt_ref[p // 2, a + 2, :, C * (p % 2) : C * (p % 2) + C] = flat[p].T
 
 
 def weight_grad(x_ref, gt_ref, columns, scale, store):
@@ -534,12 +534,15 @@
     red1b.step(0)
     red1a.step(1)
     receive_faces(3, xhid)
-    red1b.step(1)
 
     def last_done(a, v):
         unpair_plane(out_s, a, maskb[a].astype(F32) * v)
 
     def last_between(q):
+        @pl.when(q == 0)
+        def _():
+            red1b.step(1)
+
         @pl.when(q == 1)
         def _():
             red2a.step(3)

time: 84.7 us -> 86.3 us (1.019)
  Pallas kernels: 83.7 us -> 85.4 us
    pallas_call x1, Pallas kernels: 79.9 us -> 81.5 us  [body(): pl.pallas_call(functools.partial(kernel, scale), out_shape=tuple(parts),...]
where the time goes in v7:
time: 86.3 us; the launch traced here: 86.2 us
  Pallas kernels  85.4 us (99%)
    pallas_call x1, Pallas kernels, body(): pl.pallas_call(functools.partial(kernel, scale), out_shape=tuple(parts),...  81.5 us
    pallas_call x1, Pallas kernels, body(): pl.pallas_call(finish, out_shape=(*parts[:2], jax.ShapeDtypeStruct((27, C...  3.85 us

profile of v7, /device:TPU:1, one launch (start us, length us, event | category | flops | bytes accessed | tf_op | source)
XLA Modules:
  0.0 86.2 jit_solution(15153662539261735967)
XLA Ops:
  0.6 81.5 %bricks.1 = (bf16[4,2,8,8,8,128]{5,4,3,2,1,0:T(8,128)(2,1)}, bf16[4,2,8,8,8,128]{5,4,3,2,1,0:T(8,128)(2,1)}, bf16[2,16,6,8,128]{4,3,2,1,0:T(8,128)(2,1)}, bf16[2...) custom-call(bf16[8,8,8,8,128]{4,3,2,1,0:T(8,128)(2,1)} %bitcast.4, ...), custom_call_target="tpu_custom_call" | custom-call | tf_op jit(solution)/shard_map/bricks/pallas_call | solution.py:635
  82.2 3.8 %outputs.1 = (bf16[4,2,8,8,8,128]{5,4,3,2,1,0:T(8,128)(2,1)}, bf16[4,2,8,8,8,128]{5,4,3,2,1,0:T(8,128)(2,1)}, f32[27,128,128]{2,1,0:T(8,128)}, f32[27,128,128]{2,1,0:T(8,128)}) custom-call(bf16[4,2,8,8,8,128]{5,4,3,2,1,0:T(8,128)(2,1)} %get-tuple-element.14.out_t, bf16[4,2,8,8,8,128]{5,4,3,2,1,0:T(8,128)(2,1)} %get-tuple-element.15.gin_t, ...), custom_call_target="tpu_custom_call" | custom-call | tf_op jit(solution)/shard_map/outputs/pallas_call | solution.py:669

commit v8 on v7

--- a/solution.py
+++ b/solution.py
@@ -529,29 +529,22 @@
 
     weight_grad(xin, gt, LEFT_COLUMNS, scale, lambda q, c, v: red1a.put(4 * (2 - q) + c, v))
     red1a.step(0)
-    red2b.step(2)
     weight_grad(xin, gt, RIGHT_COLUMNS, scale, lambda q, c, v: red1b.put(5 * (2 - q) + c - 4, v))
     red1b.step(0)
     red1a.step(1)
+    red1b.step(1)
+    red2b.step(2)
     receive_faces(3, xhid)
 
     def last_done(a, v):
         unpair_plane(out_s, a, maskb[a].astype(F32) * v)
 
     def last_between(q):
-        @pl.when(q == 0)
-        def _():
-            red1b.step(1)
-
         @pl.when(q == 1)
         def _():
-            red2a.step(3)
+            red1a.step(2)
 
         @pl.when(q == 2)
-        def _():
-            red1a.step(2)
-
-        @pl.when(q == 3)
         def _():
             red1b.step(2)
 
@@ -564,8 +557,9 @@
         )
     ]
     stores[0].start()
+    red2a.step(3)
+    red1a.step(3)
     red2b.step(3)
-    red1a.step(3)
     red2a.step(4)
     stores[1].start()
     red2b.step(4)

time: 86.3 us -> 84.8 us (0.983)
  Pallas kernels: 85.4 us -> 83.8 us
    pallas_call x1, Pallas kernels: 81.5 us -> 79.9 us  [body(): pl.pallas_call(functools.partial(kernel, scale), out_shape=tuple(parts),...]
where the time goes in v8:
time: 84.8 us; the launch traced here: 84.6 us
  Pallas kernels  83.8 us (99%)
    pallas_call x1, Pallas kernels, body(): pl.pallas_call(functools.partial(kernel, scale), out_shape=tuple(parts),...  79.9 us
    pallas_call x1, Pallas kernels, body(): pl.pallas_call(finish, out_shape=(*parts[:2], jax.ShapeDtypeStruct((27, C...  3.85 us

profile of v8, /device:TPU:1, one launch (start us, length us, event | category | flops | bytes accessed | tf_op | source)
XLA Modules:
  0.0 84.6 jit_solution(4131742148288703681)
XLA Ops:
  0.6 79.9 %bricks.1 = (bf16[4,2,8,8,8,128]{5,4,3,2,1,0:T(8,128)(2,1)}, bf16[4,2,8,8,8,128]{5,4,3,2,1,0:T(8,128)(2,1)}, bf16[2,16,6,8,128]{4,3,2,1,0:T(8,128)(2,1)}, bf16[2...) custom-call(bf16[8,8,8,8,128]{4,3,2,1,0:T(8,128)(2,1)} %bitcast.4, ...), custom_call_target="tpu_custom_call" | custom-call | tf_op jit(solution)/shard_map/bricks/pallas_call | solution.py:629
  80.6 3.8 %outputs.1 = (bf16[4,2,8,8,8,128]{5,4,3,2,1,0:T(8,128)(2,1)}, bf16[4,2,8,8,8,128]{5,4,3,2,1,0:T(8,128)(2,1)}, f32[27,128,128]{2,1,0:T(8,128)}, f32[27,128,128]{2,1,0:T(8,128)}) custom-call(bf16[4,2,8,8,8,128]{5,4,3,2,1,0:T(8,128)(2,1)} %get-tuple-element.14.out_t, bf16[4,2,8,8,8,128]{5,4,3,2,1,0:T(8,128)(2,1)} %get-tuple-element.15.gin_t, ...), custom_call_target="tpu_custom_call" | custom-call | tf_op jit(solution)/shard_map/outputs/pallas_call | solution.py:663

commit v9 on v8

--- a/solution.py
+++ b/solution.py
@@ -319,11 +319,17 @@
         else:
             each(0, lambda d: self.forward(d).wait_recv())
 
-    def drain(self):
+    def drain_scatter(self):
         self.pair().wait_send()
 
         def body(d, _):
             self.scatter(d).wait_send()
+            return 0
+
+        lax.fori_loop(1, 16, body, 0)
+
+    def drain_gather(self):
+        def body(d, _):
             self.gather(d).wait_send()
             self.forward(d).wait_send()
             return 0
@@ -564,16 +570,20 @@
     stores[1].start()
     red2b.step(4)
     stores[2].start()
+    for n in range(4):
+        for c in face_copies(n):
+            c.wait_send()
+    for red in reductions:
+        red.drain_scatter()
+    red2a.drain_gather()
+    red2b.drain_gather()
     red1b.step(3)
     red1a.step(4)
     stores[3].start()
+    red1a.drain_gather()
     red1b.step(4)
     stores[4].start()
-    for n in range(4):
-        for c in face_copies(n):
-            c.wait_send()
-    for red in (red2a, red2b, red1a, red1b):
-        red.drain()
+    red1b.drain_gather()
     for c in stores:
         c.wait()
 
@@ -607,9 +617,10 @@
             for c in RIGHT_COLUMNS:
                 order(right, 5 * k + c - 4, dst, 9 * k + c)
         writes[i].start()
-    for i in (4, 5):
-        reads[i].wait()
-        writes[i - 2].start()
+        if i == 0:
+            for n in (4, 5):
+                reads[n].wait()
+                writes[n - 2].start()
     for c in writes:
         c.wait()
 

time: 84.8 us -> 84.8 us (level)
  no operation moved by 1% of the time
where the time goes in v9:
time: 84.8 us; the launch traced here: 84.6 us
  Pallas kernels  83.8 us (99%)
    pallas_call x1, Pallas kernels, body(): pl.pallas_call(functools.partial(kernel, scale), out_shape=tuple(parts),...  79.9 us
    pallas_call x1, Pallas kernels, body(): pl.pallas_call(finish, out_shape=(*parts[:2], jax.ShapeDtypeStruct((27, C...  3.85 us

profile of v9, /device:TPU:1, one launch (start us, length us, event | category | flops | bytes accessed | tf_op | source)
XLA Modules:
  0.0 84.6 jit_solution(10974795829918820823)
XLA Ops:
  0.6 79.9 %bricks.1 = (bf16[4,2,8,8,8,128]{5,4,3,2,1,0:T(8,128)(2,1)}, bf16[4,2,8,8,8,128]{5,4,3,2,1,0:T(8,128)(2,1)}, bf16[2,16,6,8,128]{4,3,2,1,0:T(8,128)(2,1)}, bf16[2...) custom-call(bf16[8,8,8,8,128]{4,3,2,1,0:T(8,128)(2,1)} %bitcast.4, ...), custom_call_target="tpu_custom_call" | custom-call | tf_op jit(solution)/shard_map/bricks/pallas_call | solution.py:640
  80.6 3.8 %outputs.1 = (bf16[4,2,8,8,8,128]{5,4,3,2,1,0:T(8,128)(2,1)}, bf16[4,2,8,8,8,128]{5,4,3,2,1,0:T(8,128)(2,1)}, f32[27,128,128]{2,1,0:T(8,128)}, f32[27,128,128]{2,1,0:T(8,128)}) custom-call(bf16[4,2,8,8,8,128]{5,4,3,2,1,0:T(8,128)(2,1)} %get-tuple-element.14.out_t, bf16[4,2,8,8,8,128]{5,4,3,2,1,0:T(8,128)(2,1)} %get-tuple-element.15.gin_t, ...), custom_call_target="tpu_custom_call" | custom-call | tf_op jit(solution)/shard_map/outputs/pallas_call | solution.py:674
